TPU v7x, 256 devices: a whole 4x4x8 slice. The times are simulated.
256 devices in a mesh: span: 16 (over z, x_hi), sp: 8 (over y, x_lo), fsdp: 2 (over core).
Axes of the slice: x: 4 (x_hi: 2, x_lo: 2; x = x_hi * 2 + x_lo), y: 4, z: 8, core: 2. Of those that a mesh axis runs over, the one named last changes fastest.
Arguments:
- query_pre: bfloat16 [2, 16384, 3072], P('fsdp', ('span', 'sp')), may hold values from -12 to 12
- key_pre: bfloat16 [2, 16384, 3072], P('fsdp', ('span', 'sp')), may hold values from -12 to 12
- values: bfloat16 [2, 16384, 3072], P('fsdp', ('span', 'sp')), may hold values from -6 to 6
- cotangent: bfloat16 [2, 16384, 3072], P('fsdp', ('span', 'sp')), may hold values from -6 to 6
- gains: float32 [2, 3072], P(None, 'fsdp'), may hold values from 0.5 to 1.5
- frame_span: int32 [2, 16384], P('fsdp', 'span'), may hold values from 0 to 31, as said below
- denoise_steps: int32 [2, 32], P('fsdp'), may hold values from 1 to 4
Outputs:
- query_grad: bfloat16 [2, 16384, 3072], P('fsdp', ('span', 'sp'))
- key_grad: bfloat16 [2, 16384, 3072], P('fsdp', ('span', 'sp'))
- value_grad: bfloat16 [2, 16384, 3072], P('fsdp', ('span', 'sp'))
- gain_grad: float32 [2, 3072], P(None, 'fsdp')
Inputs may be any that keep to these rules, and one draw needn't show every extreme that they name: `frame_span`: never falls along a video. Group g (tokens g * 1024 to (g + 1) * 1024 - 1) holds frame spans 2 g and 2 g + 1, each from a quarter to three quarters of the group's tokens.
All inputs are finite; a program needn't handle non-finite values.
Results may differ from a plain program's by a relative error of at most 0.0081.
The roundings to bfloat16 on the way count: a program that leaves them out, or rounds other values in their place, can miss the bound.
Values may be sent and summed in bfloat16 or wider, within the bound.
No kernel may reach another device: no remote copies, remote signals or barrier semaphores. Data moves between devices by JAX's collectives and lax.ppermute only.
A program may use at most 128 MiB of HBM per device.

v0:
```python
import jax
import jax.numpy as jnp
from jax import lax
from jax.sharding import PartitionSpec as P

HDIM = 128


EPSILON = 1e-06
NEGATIVE = -1e30


def from_behind(value, axis, steps):
    count = lax.axis_size(axis)
    first, last = (max(0, -steps), min(count, count - steps))
    return lax.ppermute(value, axis, [(source, source + steps) for source in range(first, last)])


def normed(raw_rows, gain_row):
    wide = raw_rows.astype(jnp.float32)
    inverse_rms = lax.rsqrt(jnp.mean(wide * wide, axis=-1, keepdims=True) + EPSILON)
    normal_rows = wide * inverse_rms
    return (normal_rows, inverse_rms, (normal_rows * gain_row).astype(jnp.bfloat16))


def norm_backward(grad_rows, normal_rows, inverse_rms, gain_row):
    upstream = grad_rows.astype(jnp.float32)
    scaled = upstream * gain_row
    inner = jnp.mean(scaled * normal_rows, axis=-1, keepdims=True)
    result = (inverse_rms * (scaled - normal_rows * inner)).astype(jnp.bfloat16)
    return (result, jnp.sum(upstream * normal_rows, axis=0))


def across(left, right):
    return lax.dot_general(
        left, right, (((1,), (1,)), ((), ())), preferred_element_type=jnp.float32
    )


def downward(left, right):
    return lax.dot_general(
        left, right, (((0,), (0,)), ((), ())), preferred_element_type=jnp.float32
    )


def head_grads(
    query_head, grad_head, key_joined, value_joined, joined_mask, step_weight, own_width
):
    score_scale = HDIM ** (-0.5)
    scores = across(query_head, key_joined) * score_scale
    masked = jnp.where(joined_mask, scores, NEGATIVE)
    row_max = jnp.max(masked, axis=1)
    row_total = jnp.sum(jnp.exp(masked - row_max[:, None]), axis=1)
    log_total = row_max + jnp.log(row_total)
    grad_prob = across(grad_head, value_joined)
    probs = jnp.where(joined_mask, jnp.exp(scores - log_total[:, None]), 0.0)
    row_delta = jnp.sum(probs * grad_prob, axis=1)
    factor = step_weight[:, None]
    sgrad = (factor * probs * (grad_prob - row_delta[:, None])).astype(jnp.bfloat16)
    weights = (factor * probs).astype(jnp.bfloat16)
    query_part = jnp.dot(sgrad, key_joined, preferred_element_type=jnp.float32) * score_scale
    key_own_grad = downward(sgrad[:, :own_width], query_head) * score_scale
    value_own_grad = downward(weights[:, :own_width], grad_head)
    return (
        query_part,
        key_own_grad,
        value_own_grad,
        sgrad[:, own_width:],
        weights[:, own_width:],
        log_total,
        row_delta,
    )


def on_device(query_pre, key_pre, values, cotangent, gains, frame_span, denoise_steps):
    gain_full = lax.all_gather(gains, "fsdp", axis=1, tiled=True)
    q_normal, q_inverse, q_ready = normed(query_pre[0], gain_full[0])
    k_normal, k_inverse, k_ready = normed(key_pre[0], gain_full[1])
    heads_query, heads_key, heads_value, heads_grad = (
        lax.all_to_all(q_ready, "sp", split_axis=1, concat_axis=0, tiled=True),
        lax.all_to_all(k_ready, "sp", split_axis=1, concat_axis=0, tiled=True),
        lax.all_to_all(values[0], "sp", split_axis=1, concat_axis=0, tiled=True),
        lax.all_to_all(cotangent[0], "sp", split_axis=1, concat_axis=0, tiled=True),
    )
    head_count = heads_query.shape[1] // HDIM
    own_width = heads_query.shape[0]
    span_ids = frame_span[0]
    step_table = denoise_steps[0].astype(jnp.float32)
    matches = span_ids[:, None] == lax.iota(jnp.int32, step_table.shape[0])[None, :]
    step_weight = jnp.sum(jnp.where(matches, step_table[None, :], 0.0), axis=1)
    group_index = lax.axis_index("span")
    key_prev, value_prev = from_behind((heads_key, heads_value), "span", 1)
    own_mask = span_ids[None, :] <= span_ids[:, None]
    prev_open = group_index > 0
    prev_mask = jnp.broadcast_to(prev_open, own_mask.shape)
    joined_mask = jnp.concatenate([own_mask, prev_mask], axis=1)
    key_joined_all = jnp.concatenate([heads_key, key_prev], axis=0)
    value_joined_all = jnp.concatenate([heads_value, value_prev], axis=0)
    query_parts = []
    key_parts = []
    value_parts = []
    sgrad_list = []
    weight_list = []
    total_list = []
    delta_list = []
    for head_index in range(head_count):
        first = head_index * HDIM
        last = first + HDIM
        outcome = head_grads(
            heads_query[:, first:last],
            heads_grad[:, first:last],
            key_joined_all[:, first:last],
            value_joined_all[:, first:last],
            joined_mask,
            step_weight,
            own_width,
        )
        query_parts.append(outcome[0])
        key_parts.append(outcome[1])
        value_parts.append(outcome[2])
        sgrad_list.append(outcome[3])
        weight_list.append(outcome[4])
        total_list.append(outcome[5])
        delta_list.append(outcome[6])
    query_attn = jnp.concatenate(query_parts, axis=1)
    key_own = jnp.concatenate(key_parts, axis=1)
    value_own = jnp.concatenate(value_parts, axis=1)
    key_terms = []
    value_terms = []
    for head_index in range(head_count):
        first = head_index * HDIM
        last = first + HDIM
        key_terms.append(
            downward(sgrad_list[head_index], heads_query[:, first:last]) * HDIM ** (-0.5)
        )
        value_terms.append(downward(weight_list[head_index], heads_grad[:, first:last]))
    key_back, value_back = from_behind(
        (jnp.concatenate(key_terms, axis=1), jnp.concatenate(value_terms, axis=1)), "span", -1
    )
    key_attn = key_own + key_back
    value_attn = value_own + value_back
    query_tokens, key_tokens, value_tokens = (
        lax.all_to_all(
            query_attn.astype(jnp.bfloat16), "sp", split_axis=0, concat_axis=1, tiled=True
        ),
        lax.all_to_all(
            key_attn.astype(jnp.bfloat16), "sp", split_axis=0, concat_axis=1, tiled=True
        ),
        lax.all_to_all(
            value_attn.astype(jnp.bfloat16), "sp", split_axis=0, concat_axis=1, tiled=True
        ),
    )
    query_back, query_gain = norm_backward(query_tokens, q_normal, q_inverse, gain_full[0])
    key_back_rows, key_gain = norm_backward(key_tokens, k_normal, k_inverse, gain_full[1])
    partial_value = jnp.stack([query_gain, key_gain])
    summed = lax.psum(partial_value, ("span", "sp"))
    gain_grad = lax.psum_scatter(summed, "fsdp", scatter_dimension=1, tiled=True)
    return (query_back[None], key_back_rows[None], value_tokens[None], gain_grad)


def solution(mesh):
    placed = (
        P("fsdp", ("span", "sp"), None),
        P("fsdp", ("span", "sp"), None),
        P("fsdp", ("span", "sp"), None),
        P("fsdp", ("span", "sp"), None),
        P(None, "fsdp"),
        P("fsdp", "span"),
        P("fsdp", None),
    )
    return jax.shard_map(
        on_device,
        mesh=mesh,
        in_specs=placed,
        out_specs=(
            P("fsdp", ("span", "sp"), None),
            P("fsdp", ("span", "sp"), None),
            P("fsdp", ("span", "sp"), None),
            P(None, "fsdp"),
        ),
        check_vma=False,
    )
```

profile of v0, /device:TPU:0, one launch (start us, length us, event | category | flops | bytes accessed | tf_op | source)
XLA Modules:
  0.0 1030.9 jit_solution(12937883028764885410)
XLA Ops:
  7.2 2.4 copy.78
  9.5 4.2 all-to-all-start.2
  18.8 7.4 all-to-all-done.2
  26.2 3.5 all-to-all-start.1
  29.8 2.3 copy.80
  32.1 9.4 all-to-all-done.1
  41.5 4.3 all-to-all-start.3
  46.3 5.9 collective-permute-start
  53.5 6.6 all-to-all-done.3
  60.1 4.2 all-to-all-start
  65.1 2.3 copy.79
  67.4 2.3 copy.81
  69.7 2.9 collective-permute-start.1
  72.6 12.8 %all-to-all-done = bf16[128,8,384]{2,0,1:T(8,128)(2,1)} async-done(((bf16[128,8,384]{2,0,1:T(8,128)(2,1)}), bf16[128,8,384]{2,0,1:T(8,128)(2,1)}, u32[]{:S(2)}, u32[]{:S(2)}) %all-to-all-start) | async-done | bytes 786464 | tf_op jit(solution)/shard_map/all_to_all | solution.py:80
  85.4 2.3 fusion.75
  87.7 2.7 fusion.82
  90.4 8.7 fusion.9
  99.1 8.6 exponential_reduce_fusion.2
  107.7 5.4 fusion.68
  113.1 5.4 fusion.61
  118.6 20.2 %fusion.6 = (f32[1024]{0:T(1024)S(1)}, f32[1024]{0:T(1024)S(1)}, f32[1024]{0:T(1024)S(1)}, f32[2048,1024]{0,1:T(8,128)}) fusion(f32[1024]{0:T(1024)S(1)} %log_add_fusion.2, f32[1024,2048]{1,0:T(8,128)} %get-tuple-element.37, pred[1024,1024]{1,0:T(32,128)(4,1)S(1)} %broadcast_compare_fusion, pred[]{:T(512)S(6)} %gt.3, f32[2048,1024]{0,1:T(8,128)} %fusion.68, ...), kind=kOutput, calls=%fused_computation.18 | convolution fusion | flops 569373696 | bytes 53239808 | tf_op jit(solution)/shard_map/dot_general | solution.py:35
  138.8 12.6 %multiply_convert_fusion.2 = (bf16[1024,2048]{1,0:T(8,128)(2,1)S(1)}, bf16[1024,2048]{1,0:T(8,128)(2,1)S(1)}, bf16[1024,2048]{1,0:T(8,128)(2,1)S(1)}, bf16[1024,2048]{1,0:T(8,128)(2,1)S(1)}) fusion(f32[1024]{0:T(1024)S(1)} %select_reduce_fusion, f32[1024]{0:T(1024)S(1)} %log_add_fusion.2, f32[1024,2048]{1,0:T(8,128)} %get-tuple-element.37, ...), kind=kLoop, calls=%fused_computation.26 | loop fusion | flops 33554432 | bytes 51400704 | tf_op jit(solution)/shard_map/convert_element_type | solution.py:60
  157.0 2.6 fusion.47
  159.6 3.3 fusion.38
  162.9 2.5 fusion.53
  165.4 2.5 fusion.44
  167.9 4.9 multiply_convert_fusion.1
  172.8 3.2 fusion.50
  176.0 3.5 fusion.56
  179.4 2.3 fusion.58
  181.8 2.2 fusion.57
  185.0 4.3 all-to-all-start.4
  189.3 2.8 pad_maximum_fusion
  198.6 2.2 fusion.20
  200.8 2.5 fusion.41
  208.8 2.6 reshape.278
  211.4 21.7 %collective-permute-done.2 = f32[1024,384]{1,0:T(8,128)} collective-permute-done((f32[1024,384]{1,0:T(8,128)}, f32[1024,384]{1,0:T(8,128)}, u32[]{:S(2)}, u32[]{:S(2)}) %collective-permute-start.2) | collective-permute-done | bytes 1572896 | tf_op jit(solution)/shard_map/ppermute | solution.py:16
  233.1 2.6 fusion.36
  235.6 5.6 all-to-all-start.5
  241.2 2.7 multiply_convert_fusion.4
  243.9 19.0 %collective-permute-done.3 = f32[1024,384]{0,1:T(8,128)} collective-permute-done((f32[1024,384]{0,1:T(8,128)}, f32[1024,384]{0,1:T(8,128)}, u32[]{:S(2)}, u32[]{:S(2)}) %collective-permute-start.3) | collective-permute-done | bytes 1572896 | tf_op jit(solution)/shard_map/ppermute | solution.py:16
  262.9 2.9 copy_bitcast_fusion
  265.8 10.1 all-to-all-done.5
  276.0 4.2 all-to-all-start.6
  287.9 5.7 all-to-all-done.6
  293.6 2.3 copy.94
  295.9 37.5 %reduce-scatter.4.cloned.1.call-done = f32[1536,2]{1,0:T(8,128)} async-done(((f32[3072,2]{1,0:T(8,128)}), f32[1536,2]{1,0:T(8,128)}) %reduce-scatter.4.cloned.1.call-update) | async-done | bytes 12304
  334.8 688.9 %psum.8 = f32[2,1536]{1,0:T(2,128)} all-reduce(f32[2,1536]{1,0:T(2,128)S(1)} %copy.105), channel_id=1, replica_groups=mesh['span'=16,'sp'=8,'fsdp'=2] {'span','sp'}, use_global_device_ids=true, to_apply=%region_16.17 | all-reduce | flops 3072 | bytes 24576 | tf_op jit(solution)/shard_map/psum | solution.py:156
  (98 shorter events, 35.1 us)
Async XLA Ops:
  7.2 10.0 copy-start.7
  9.5 16.7 %all-to-all-start.2 = ((bf16[128,8,384]{0,2,1:T(8,128)(2,1)}), bf16[128,8,384]{0,2,1:T(8,128)(2,1)}, u32[]{:S(2)}, u32[]{:S(2)}) async-start(bf16[128,8,384]{0,2,1:T(8,128)(2,1)} %bitcast.7), calls=%async_computation.2 | async-start | bytes 1572864 | tf_op jit(solution)/shard_map/all_to_all | solution.py:82
  17.2 28.6 %copy-start.5 = (bf16[1,128,3072]{2,1,0:T(8,128)(2,1)S(1)}, bf16[1,128,3072]{2,1,0:T(8,128)(2,1)}, u32[]{:S(2)}) copy-start(bf16[1,128,3072]{2,1,0:T(8,128)(2,1)} %param.7) | copy-start | bytes 2359300
  26.2 15.2 %all-to-all-start.1 = ((bf16[128,8,384]{2,0,1:T(8,128)(2,1)}), bf16[128,8,384]{2,0,1:T(8,128)(2,1)S(1)}, u32[]{:S(2)}, u32[]{:S(2)}) async-start(bf16[128,8,384]{2,0,1:T(8,128)(2,1)} %multiply_convert_fusion.5), calls=%async_computation.1 | async-start | bytes 1572864 | tf_op jit(solution)/shard_map/all_to_all | solution.py:81
  41.5 22.9 %copy-start.20 = (s32[1,32]{1,0:T(1,128)S(1)}, s32[1,32]{1,0:T(1,128)}, u32[]{:S(2)}) copy-start(s32[1,32]{1,0:T(1,128)} %param.13) | copy-start | bytes 388
  41.5 22.9 %copy-start.19 = (s32[1,1024]{1,0:T(1,128)S(1)}, s32[1,1024]{1,0:T(1,128)}, u32[]{:S(2)}) copy-start(s32[1,1024]{1,0:T(1,128)} %param.12) | copy-start | bytes 12292
  41.5 18.7 %all-to-all-start.3 = ((bf16[128,8,384]{0,2,1:T(8,128)(2,1)}), bf16[128,8,384]{0,2,1:T(8,128)(2,1)}, u32[]{:S(2)}, u32[]{:S(2)}) async-start(bf16[128,8,384]{0,2,1:T(8,128)(2,1)} %bitcast.118), calls=%async_computation.3 | async-start | bytes 1572864 | tf_op jit(solution)/shard_map/all_to_all | solution.py:83
  46.0 6.1 copy-start.2
  46.3 39.1 %collective-permute-start = (bf16[1024,384]{1,0:T(8,128)(2,1)S(1)}, bf16[1024,384]{1,0:T(8,128)(2,1)}, u32[]{:S(2)}, u32[]{:S(2)}) collective-permute-start(bf16[1024,384]{1,0:T(8,128)(2,1)S(1)} %bitcast.91), channel_id=1, source_target_pairs={{0,16},{16,32},{32,48},{48,64},{64,80},{80,96},{96,112},{112,128},... | collective-permute-start | bytes 2359304 | tf_op jit(solution)/shard_map/ppermute | solution.py:16
  60.1 25.3 %all-to-all-start = ((bf16[128,8,384]{2,0,1:T(8,128)(2,1)}), bf16[128,8,384]{2,0,1:T(8,128)(2,1)}, u32[]{:S(2)}, u32[]{:S(2)}) async-start(bf16[128,8,384]{2,0,1:T(8,128)(2,1)} %multiply_convert_fusion.6), calls=%async_computation | async-start | bytes 1572864 | tf_op jit(solution)/shard_map/all_to_all | solution.py:80
  69.7 38.0 %collective-permute-start.1 = (bf16[1024,384]{1,0:T(8,128)(2,1)}, bf16[1024,384]{1,0:T(8,128)(2,1)}, u32[]{:S(2)}, u32[]{:S(2)}) collective-permute-start(bf16[1024,384]{1,0:T(8,128)(2,1)} %bitcast.102), channel_id=1, source_target_pairs={{0,16},{16,32},{32,48},{48,64},{64,80},{80,96},{96,112},{112,128},... | collective-permute-start | bytes 2359304 | tf_op jit(solution)/shard_map/ppermute | solution.py:16
  87.7 11.4 %copy-start.1 = (f32[1024,2048]{1,0:T(8,128)}, f32[1024,2048]{1,0:T(8,128)S(1)}, u32[]{:S(2)}) copy-start(f32[1024,2048]{1,0:T(8,128)S(1)} %fusion.75) | copy-start | bytes 25165828
  90.4 8.7 copy-start
  99.1 8.6 copy-start.4
  99.1 8.6 copy-start.13
  138.8 12.6 %copy-start.14 = (bf16[8,128,384]{2,1,0:T(8,128)(2,1)S(1)}, bf16[8,128,384]{2,1,0:T(8,128)(2,1)}, u32[]{:S(2)}) copy-start(bf16[8,128,384]{2,1,0:T(8,128)(2,1)} %copy.81) | copy-start | bytes 2359300
  151.4 5.6 copy-start.9
  153.0 14.8 %slice-start.2 = ((s8[8388608]{0:T(1024)(128)(4,1)}), s8[4194304]{0:T(1024)(128)(4,1)S(1)}, s32[]{:S(2)}) async-start(s8[8388608]{0:T(1024)(128)(4,1)} %bitcast.89), calls=%async_computation.11 | async-start | bytes 8388608
  155.6 12.2 %slice-start = ((s8[8388608]{0:T(1024)(128)(4,1)}), s8[4194304]{0:T(1024)(128)(4,1)S(1)}, s32[]{:S(2)}) async-start(s8[8388608]{0:T(1024)(128)(4,1)} %bitcast.87), calls=%async_computation.9 | async-start | bytes 8388608
  157.0 10.9 %slice-start.3 = ((s8[8388608]{0:T(1024)(128)(4,1)}), s8[4194304]{0:T(1024)(128)(4,1)S(1)}, s32[]{:S(2)}) async-start(s8[8388608]{0:T(1024)(128)(4,1)} %bitcast.89), calls=%async_computation.12 | async-start | bytes 8388608
  159.6 8.3 slice-start.1
  179.4 2.4 copy-start.10
  185.0 10.5 %copy-start.17 = (f32[1024,128]{0,1:T(8,128)S(1)}, f32[1024,128]{0,1:T(8,128)}, u32[]{:S(2)}) copy-start(f32[1024,128]{0,1:T(8,128)} %fusion.16) | copy-start | bytes 1572868
  185.0 10.5 %copy-start.18 = (f32[1024,128]{0,1:T(8,128)S(1)}, f32[1024,128]{0,1:T(8,128)}, u32[]{:S(2)}) copy-start(f32[1024,128]{0,1:T(8,128)} %fusion.12) | copy-start | bytes 1572868
  185.0 18.3 %all-to-all-start.4 = ((bf16[8,128,384]{2,1,0:T(8,128)(2,1)}), bf16[8,128,384]{2,1,0:T(8,128)(2,1)}, u32[]{:S(2)}, u32[]{:S(2)}) async-start(bf16[8,128,384]{2,1,0:T(8,128)(2,1)} %pad_maximum_fusion.2), calls=%async_computation.4 | async-start | bytes 1572864 | tf_op jit(solution)/shard_map/all_to_all | solution.py:143
  189.3 9.2 copy-start.12
  192.1 41.0 %collective-permute-start.2 = (f32[1024,384]{1,0:T(8,128)}, f32[1024,384]{1,0:T(8,128)}, u32[]{:S(2)}, u32[]{:S(2)}) collective-permute-start(f32[1024,384]{1,0:T(8,128)} %pad_maximum_fusion), channel_id=1, source_target_pairs={{16,0},{32,16},{48,32},{64,48},{80,64},{96,80},{112,96},{128,112},... | collective-permute-start | bytes 4718600 | tf_op jit(solution)/shard_map/ppermute | solution.py:16
  195.5 5.3 copy-start.11
  196.8 6.6 copy-start.3
  196.8 66.1 %collective-permute-start.3 = (f32[1024,384]{0,1:T(8,128)}, f32[1024,384]{0,1:T(8,128)}, u32[]{:S(2)}, u32[]{:S(2)}) collective-permute-start(f32[1024,384]{0,1:T(8,128)} %pad_maximum_fusion.1), channel_id=1, source_target_pairs={{16,0},{32,16},{48,32},{64,48},{80,64},{96,80},{112,96},{128,112},... | collective-permute-start | bytes 4718600 | tf_op jit(solution)/shard_map/ppermute | solution.py:16
  205.4 27.7 %copy-start.15 = (f32[1024,128]{1,0:T(8,128)S(1)}, f32[1024,128]{1,0:T(8,128)}, u32[]{:S(2)}) copy-start(f32[1024,128]{1,0:T(8,128)} %fusion.38) | copy-start | bytes 1572868
  205.4 27.7 %copy-start.16 = (f32[1024,128]{1,0:T(8,128)S(1)}, f32[1024,128]{1,0:T(8,128)}, u32[]{:S(2)}) copy-start(f32[1024,128]{1,0:T(8,128)} %fusion.44) | copy-start | bytes 1572868
  208.8 32.5 %copy-start.6 = (bf16[1,128,3072]{2,1,0:T(8,128)(2,1)S(1)}, bf16[1,128,3072]{2,1,0:T(8,128)(2,1)}, u32[]{:S(2)}) copy-start(bf16[1,128,3072]{2,1,0:T(8,128)(2,1)} %param.7) | copy-start | bytes 2359300
  235.6 40.3 %all-to-all-start.5 = ((bf16[8,128,384]{2,1,0:T(8,128)(2,1)}), bf16[8,128,384]{2,1,0:T(8,128)(2,1)S(1)}, u32[]{:S(2)}, u32[]{:S(2)}) async-start(bf16[8,128,384]{2,1,0:T(8,128)(2,1)} %bitcast.119), calls=%async_computation.5 | async-start | bytes 1572864 | tf_op jit(solution)/shard_map/all_to_all | solution.py:146
  276.0 17.6 %all-to-all-start.6 = ((bf16[8,128,384]{1,2,0:T(8,128)(2,1)}), bf16[8,128,384]{1,2,0:T(8,128)(2,1)}, u32[]{:S(2)}, u32[]{:S(2)}) async-start(bf16[8,128,384]{1,2,0:T(8,128)(2,1)} %copy_bitcast_fusion), calls=%async_computation.6 | async-start | bytes 1572864 | tf_op jit(solution)/shard_map/all_to_all | solution.py:149
  280.2 53.2 %reduce-scatter.4.cloned.1.call-start = ((), (), s32[]{:S(2)}) async-start(), calls=%async_computation.8 | async-start | bytes 2359296
  281.3 5.3 copy-start.8
Sparse Core Ops, SparseCore 0:
  286.7 46.5 reduce-scatter.3
where the time goes:
time: 1040 us; the launch traced here: 1030 us
  blocking collectives  691 us (66%)
  waiting for transfers between devices  130 us (12%)
  matrix products  79.1 us (8%)
  other arithmetic  48.9 us (5%)
  starting transfers between devices  42.4 us (4%)
  local copies, waits for them, and re-layouts  24.5 us (2%)
  between operations  15 us (1%)
    psum x1, blocking collectives, on_device(): summed = lax.psum(partial_value, ('span', 'sp'))  689 us
    dot_general x6, matrix products, across(): lax.dot_general(left, right, (((1,), (1,)), ((), ())), preferred_element_...  44.7 us
    ppermute x4, waiting for transfers between devices, from_behind(): lax.ppermute(value, axis, [(source, source + steps) for source in range(f...  40.6 us
    unnamed x2, waiting for transfers between devices  37.5 us
    dot_general x12, matrix products, downward(): lax.dot_general(left, right, (((0,), (0,)), ((), ())), preferred_element_...  26.5 us
  transfers between devices with their start and end apart: 12, of which 9 were waited for; matrix products, arithmetic and copies ran while one was open for 7% of the time, Pallas kernels for 0%

commit v1 on v0

v1 whole, which is shorter than its diff:
```python
import functools

import jax
import jax.numpy as jnp
import numpy as np
from jax import lax
from jax.experimental import pallas as pl
from jax.experimental.pallas import tpu as pltpu
from jax.sharding import PartitionSpec as P

HDIM = 128
TOK = 128
GROUP = 1024
QTILE = 256
KCHUNK = 256
EPSILON = 1e-06
NEGATIVE = -1e30
LOG2E = 1.4426950408889634
SCALE = HDIM ** (-0.5)
F32 = jnp.float32
BF16 = jnp.bfloat16


def nt(left, right):
    return lax.dot_general(left, right, (((1,), (1,)), ((), ())), preferred_element_type=F32)


def nn(left, right):
    return lax.dot_general(left, right, (((1,), (0,)), ((), ())), preferred_element_type=F32)


def pack_kernel(heads_a, q_ref, k_ref, v_ref, g_ref, gain_ref, a_ref, b_ref):
    heads = q_ref.shape[1] // HDIM

    def put(slot, rows):
        for head in range(heads):
            piece = rows[:, head * HDIM : (head + 1) * HDIM]
            if head < heads_a:
                a_ref[head, slot] = piece
            else:
                b_ref[head - heads_a, slot] = piece

    for slot, ref in ((0, q_ref), (1, k_ref)):
        wide = ref[...].astype(F32)
        inverse = lax.rsqrt(jnp.mean(wide * wide, axis=1, keepdims=True) + EPSILON)
        put(slot, (wide * inverse * gain_ref[slot : slot + 1, :]).astype(BF16))
    put(2, v_ref[...])
    put(3, g_ref[...])


def pack(query_pre, key_pre, values, cotangent, gain_full, heads_a):
    tokens, channels = query_pre.shape
    heads_b = channels // HDIM - heads_a
    step = 32
    rows = pl.BlockSpec((step, channels), lambda i: (i, 0))
    return pl.pallas_call(
        functools.partial(pack_kernel, heads_a),
        grid=(tokens // step,),
        in_specs=[rows] * 4 + [pl.BlockSpec((2, channels), lambda i: (0, 0))],
        out_specs=[
            pl.BlockSpec((heads_a, 4, step, HDIM), lambda i: (0, 0, i, 0)),
            pl.BlockSpec((heads_b, 4, step, HDIM), lambda i: (0, 0, i, 0)),
        ],
        out_shape=[
            jax.ShapeDtypeStruct((heads_a, 4, tokens, HDIM), BF16),
            jax.ShapeDtypeStruct((heads_b, 4, tokens, HDIM), BF16),
        ],
        name="pack",
        cost_estimate=pl.CostEstimate(
            flops=10 * tokens * channels, bytes_accessed=16 * tokens * channels, transcendentals=tokens
        ),
    )(query_pre, key_pre, values, cotangent, gain_full)


def unit_kernel(
    info_ref, q_ref, g_ref, ko_ref, vo_ref, kp_ref, vp_ref,
    dq_ref, dko_ref, dvo_ref, dkp_ref, dvp_ref,
    k_ref, v_ref, kt_ref, s_ref, dp_ref, dk_ref, dv_ref,
):
    step = pl.program_id(0)
    chunks = 2 * GROUP // KCHUNK
    own_chunks = GROUP // KCHUNK

    @pl.when(step == 0)
    def _():
        k_ref[:GROUP] = ko_ref[...].reshape(GROUP, HDIM)
        k_ref[GROUP:] = kp_ref[...].reshape(GROUP, HDIM)
        v_ref[:GROUP] = vo_ref[...].reshape(GROUP, HDIM)
        v_ref[GROUP:] = vp_ref[...].reshape(GROUP, HDIM)
        kt_ref[...] = k_ref[...].T
        dk_ref[...] = jnp.zeros_like(dk_ref)
        dv_ref[...] = jnp.zeros_like(dv_ref)

    bound = info_ref[0]
    is_open = info_ref[1] > 0
    early_weight = info_ref[2].astype(F32)
    late_weight = info_ref[3].astype(F32)
    q = q_ref[...].reshape(QTILE, HDIM)
    g = g_ref[...].reshape(QTILE, HDIM)
    place = step * QTILE + lax.broadcasted_iota(jnp.int32, (1, QTILE), 1)
    early = place < bound
    reach = jnp.where(early, bound, GROUP)
    weight = jnp.where(early, early_weight, late_weight)
    factor = SCALE * LOG2E

    own_max = None
    prev_max = None
    for chunk in range(chunks):
        span = slice(chunk * KCHUNK, (chunk + 1) * KCHUNK)
        scores = nt(k_ref[span], q)
        if 0 < chunk < own_chunks:
            row = chunk * KCHUNK + lax.broadcasted_iota(jnp.int32, (KCHUNK, QTILE), 0)
            scores = jnp.where(row < reach, scores, NEGATIVE)
        s_ref[span] = scores
        top = jnp.max(scores, axis=0, keepdims=True)
        if chunk < own_chunks:
            own_max = top if own_max is None else jnp.maximum(own_max, top)
        else:
            prev_max = top if prev_max is None else jnp.maximum(prev_max, top)
    row_max = jnp.maximum(own_max, jnp.where(is_open, prev_max, NEGATIVE)) * factor
    prev_shift = jnp.where(is_open, row_max, -NEGATIVE)
    total = jnp.zeros((1, QTILE), F32)
    inner = jnp.zeros((1, QTILE), F32)
    for chunk in range(chunks):
        span = slice(chunk * KCHUNK, (chunk + 1) * KCHUNK)
        shift = row_max if chunk < own_chunks else prev_shift
        probs = jnp.exp2(s_ref[span] * factor - shift)
        total = total + jnp.sum(probs, axis=0, keepdims=True)
        grads = nt(v_ref[span], g)
        inner = inner + jnp.sum(probs * grads, axis=0, keepdims=True)
        s_ref[span] = probs
        dp_ref[span] = grads
    over = 1.0 / total
    delta = inner * over
    scaled = weight * over
    dq_t = jnp.zeros((HDIM, QTILE), F32)
    for chunk in range(chunks):
        span = slice(chunk * KCHUNK, (chunk + 1) * KCHUNK)
        weights = s_ref[span] * scaled
        sgrad = (weights * (dp_ref[span] - delta)).astype(BF16)
        dk_ref[span] += nn(sgrad, q)
        dv_ref[span] += nn(weights.astype(BF16), g)
        dq_t = dq_t + nn(kt_ref[:, span], sgrad)
    dq_ref[...] = (dq_t * SCALE).T.astype(BF16).reshape(dq_ref.shape)

    @pl.when(step == pl.num_programs(0) - 1)
    def _():
        dko_ref[...] = dk_ref[:GROUP] * SCALE
        dvo_ref[...] = dv_ref[:GROUP]
        dkp_ref[...] = (dk_ref[GROUP:] * SCALE).astype(BF16)
        dvp_ref[...] = dv_ref[GROUP:].astype(BF16)


def unit(info, own, own_at, prev, prev_at, prev_slots, name):
    slabs = GROUP // TOK
    tiles = QTILE // TOK

    def whole(at, slot):
        return pl.BlockSpec((slabs, 1, TOK, HDIM), lambda i: (at, slot, 0, 0))

    def tiled(slot):
        first = own_at * slabs // tiles
        return pl.BlockSpec((tiles, 1, TOK, HDIM), lambda i: (first + i, slot, 0, 0))

    full = pl.BlockSpec((GROUP, HDIM), lambda i: (0, 0))
    return pl.pallas_call(
        unit_kernel,
        grid=(GROUP // QTILE,),
        in_specs=[
            pl.BlockSpec(memory_space=pltpu.SMEM),
            tiled(0), tiled(3), whole(own_at, 1), whole(own_at, 2),
            whole(prev_at, prev_slots[0]), whole(prev_at, prev_slots[1]),
        ],
        out_specs=[pl.BlockSpec((QTILE, HDIM), lambda i: (i, 0)), full, full, full, full],
        out_shape=[
            jax.ShapeDtypeStruct((GROUP, HDIM), BF16),
            jax.ShapeDtypeStruct((GROUP, HDIM), F32),
            jax.ShapeDtypeStruct((GROUP, HDIM), F32),
            jax.ShapeDtypeStruct((GROUP, HDIM), BF16),
            jax.ShapeDtypeStruct((GROUP, HDIM), BF16),
        ],
        scratch_shapes=[
            pltpu.VMEM((2 * GROUP, HDIM), BF16),
            pltpu.VMEM((2 * GROUP, HDIM), BF16),
            pltpu.VMEM((HDIM, 2 * GROUP), BF16),
            pltpu.VMEM((2 * GROUP, QTILE), F32),
            pltpu.VMEM((2 * GROUP, QTILE), F32),
            pltpu.VMEM((2 * GROUP, HDIM), F32),
            pltpu.VMEM((2 * GROUP, HDIM), F32),
        ],
        name=name,
        cost_estimate=pl.CostEstimate(
            flops=20 * GROUP * GROUP * HDIM, bytes_accessed=3 << 20, transcendentals=2 * GROUP * GROUP
        ),
    )(info, own, own, own, own, prev, prev)


def combine_kernel(groups, own_ref, *refs):
    ins, (out_ref, gain_ref) = refs[: 5 * groups], refs[5 * groups :]
    slabs = GROUP // TOK
    gain_q = jnp.zeros((1, HDIM), F32)
    gain_k = jnp.zeros((1, HDIM), F32)
    for group in range(groups):
        dq, dk, dv, dk_more, dv_more = ins[5 * group : 5 * group + 5]
        at = slice(group * slabs, (group + 1) * slabs)
        q = own_ref[at, 0].reshape(GROUP, HDIM).astype(F32)
        k = own_ref[at, 1].reshape(GROUP, HDIM).astype(F32)
        dq_all = dq[...]
        dk_all = (dk[...] + dk_more[...].astype(F32)).astype(BF16)
        dv_all = (dv[...] + dv_more[...].astype(F32)).astype(BF16)
        gain_q = gain_q + jnp.sum(dq_all.astype(F32) * q, axis=0, keepdims=True)
        gain_k = gain_k + jnp.sum(dk_all.astype(F32) * k, axis=0, keepdims=True)
        out_ref[at, 0] = dq_all.reshape(slabs, TOK, HDIM)
        out_ref[at, 1] = dk_all.reshape(slabs, TOK, HDIM)
        out_ref[at, 2] = dv_all.reshape(slabs, TOK, HDIM)
    gain_ref[0:1] = gain_q
    gain_ref[1:2] = gain_k


def combine(own, parts, name):
    groups = len(parts)
    slabs = groups * GROUP // TOK
    flat = [array for part in parts for array in part]
    full = pl.BlockSpec((GROUP, HDIM), lambda i: (0, 0))
    return pl.pallas_call(
        functools.partial(combine_kernel, groups),
        grid=(1,),
        in_specs=[pl.BlockSpec((slabs, 2, TOK, HDIM), lambda i: (0, 0, 0, 0))] + [full] * len(flat),
        out_specs=[
            pl.BlockSpec((slabs, 3, TOK, HDIM), lambda i: (0, 0, 0, 0)),
            pl.BlockSpec((2, HDIM), lambda i: (0, 0)),
        ],
        out_shape=[
            jax.ShapeDtypeStruct((slabs, 3, TOK, HDIM), BF16),
            jax.ShapeDtypeStruct((2, HDIM), F32),
        ],
        name=name,
        cost_estimate=pl.CostEstimate(
            flops=10 * groups * GROUP * HDIM, bytes_accessed=groups * GROUP * HDIM * 20, transcendentals=0
        ),
    )(own, *flat)


def finish_kernel(heads_a, heads_b, x_ref, y_ref, gain_ref, a_ref, b_ref, qg_ref, kg_ref, vg_ref):
    channels = x_ref.shape[1]

    def piece(head, slot):
        return a_ref[head, slot] if head < heads_a else b_ref[head - heads_a, slot]

    for slot, ref, out in ((0, x_ref, qg_ref), (1, y_ref, kg_ref)):
        wide = ref[...].astype(F32)
        inverse = lax.rsqrt(jnp.mean(wide * wide, axis=1, keepdims=True) + EPSILON)
        normal = wide * inverse
        up = jnp.concatenate([piece(h, slot).astype(F32) for h in range(heads_a + heads_b)], axis=1)
        scaled = up * gain_ref[slot : slot + 1, :]
        inner = jnp.sum(scaled * normal, axis=1, keepdims=True) * (1.0 / channels)
        out[...] = (inverse * (scaled - normal * inner)).astype(BF16)
    for head in range(heads_a + heads_b):
        vg_ref[:, head * HDIM : (head + 1) * HDIM] = piece(head, 2)


def finish(query_pre, key_pre, gain_full, back_a, back_b):
    tokens, channels = query_pre.shape
    heads_a, heads_b = back_a.shape[0], back_b.shape[0]
    step = 32
    rows = pl.BlockSpec((step, channels), lambda i: (i, 0))
    return pl.pallas_call(
        functools.partial(finish_kernel, heads_a, heads_b),
        grid=(tokens // step,),
        in_specs=[
            rows, rows,
            pl.BlockSpec((2, channels), lambda i: (0, 0)),
            pl.BlockSpec((heads_a, 3, step, HDIM), lambda i: (0, 0, i, 0)),
            pl.BlockSpec((heads_b, 3, step, HDIM), lambda i: (0, 0, i, 0)),
        ],
        out_specs=[rows] * 3,
        out_shape=[jax.ShapeDtypeStruct((tokens, channels), BF16)] * 3,
        name="finish",
        cost_estimate=pl.CostEstimate(
            flops=30 * tokens * channels, bytes_accessed=16 * tokens * channels, transcendentals=tokens
        ),
    )(query_pre, key_pre, gain_full, back_a, back_b)


def shifted(value, steps, count):
    first, last = (max(0, -steps), min(count, count - steps))
    return lax.ppermute(value, "span", [(source, source + steps) for source in range(first, last)])


def on_device(query_pre, key_pre, values, cotangent, gains, frame_span, denoise_steps):
    n_span, n_sp = lax.axis_size("span"), lax.axis_size("sp")
    heads_a = 2 * n_sp
    slabs = GROUP // TOK
    plane = [[first + i for i in range(heads_a)] for first in range(0, n_span * n_sp, heads_a)]
    to_plane = functools.partial(
        lax.all_to_all, axis_name=("span", "sp"), split_axis=0, concat_axis=0, tiled=True, axis_index_groups=plane
    )
    to_sp = functools.partial(lax.all_to_all, axis_name="sp", split_axis=0, concat_axis=0, tiled=True)

    span = lax.axis_index("span")
    gain_full = lax.all_gather(gains, "fsdp", axis=1, tiled=True)
    send_a, send_b = pack(query_pre[0], key_pre[0], values[0], cotangent[0], gain_full, heads_a)
    own_b = to_sp(send_b)
    own_a = to_plane(send_a)

    ids = frame_span[0]
    bound = jnp.sum((ids == ids[0]).astype(jnp.int32))
    other = lax.ppermute(
        jnp.full((8, 128), bound, F32), "span", [(i, i ^ 1) for i in range(n_span)]
    )[0, 0].astype(jnp.int32)
    odd = span % 2
    table = denoise_steps[0]
    even_bound = jnp.where(odd == 0, bound, other)
    odd_bound = jnp.where(odd == 0, other, bound)

    def info_of(limit, group):
        weights = lax.dynamic_slice(table, (2 * group,), (2,))
        return jnp.stack([limit, (group > 0).astype(jnp.int32), weights[0], weights[1]])

    even = span - odd

    prev_b = shifted(own_b[:, 1:3], 1, n_span)
    dq_b, dk_b, dv_b, dk_b_prev, dv_b_prev = unit(info_of(bound, span), own_b, 0, prev_b, 0, (0, 1), "unit_b")
    back_b = shifted(jnp.concatenate([dk_b_prev, dv_b_prev], axis=0), -1, n_span)
    out_b, gain_b = combine(own_b, [(dq_b, dk_b, dv_b, back_b[:GROUP], back_b[GROUP:])], "combine_b")
    home_b = to_sp(out_b)

    prev_a = shifted(own_a[slabs:, 1:3], 2, n_span)
    dq_o, dk_o, dv_o, dk_o_prev, dv_o_prev = unit(info_of(odd_bound, even + 1), own_a, 1, own_a, 0, (1, 2), "unit_o")
    dq_e, dk_e, dv_e, dk_e_prev, dv_e_prev = unit(info_of(even_bound, even), own_a, 0, prev_a, 0, (0, 1), "unit_e")
    back_a = shifted(jnp.concatenate([dk_e_prev, dv_e_prev], axis=0), -2, n_span)
    out_a, gain_a = combine(
        own_a,
        [(dq_e, dk_e, dv_e, dk_o_prev, dv_o_prev), (dq_o, dk_o, dv_o, back_a[:GROUP], back_a[GROUP:])],
        "combine_a",
    )
    home_a = to_plane(out_a)

    share = jnp.concatenate([gain_a, gain_b, jnp.zeros((4, HDIM), F32)], axis=0)
    share = share + lax.ppermute(share, "fsdp", [(0, 1), (1, 0)])
    reach = 2
    while reach < n_span:
        share = share + lax.ppermute(share, "span", [(i, i ^ reach) for i in range(n_span)])
        reach *= 2
    across = lax.ppermute(share, "span", [(i, i ^ 1) for i in range(n_span)])
    share = jnp.concatenate([share[:2], share[2:] + across[2:]], axis=0)
    shares = to_plane(jnp.broadcast_to(share[None], (heads_a, 8, HDIM)))
    total = jnp.stack(
        [
            jnp.concatenate([shares[:, row].reshape(-1), shares[:n_sp, 2 + row].reshape(-1)])
            for row in range(2)
        ]
    )
    half = gains.shape[1]
    mine = jnp.where(lax.axis_index("fsdp") == 0, total[:, :half], total[:, half:])
    gain_grad = mine / gains

    query_back, key_back, value_back = finish(query_pre[0], key_pre[0], gain_full, home_a, home_b)
    return (query_back[None], key_back[None], value_back[None], gain_grad)


def solution(mesh):
    rows = P("fsdp", ("span", "sp"), None)
    return jax.shard_map(
        on_device,
        mesh=mesh,
        in_specs=(rows, rows, rows, rows, P(None, "fsdp"), P("fsdp", "span"), P("fsdp", None)),
        out_specs=(rows, rows, rows, P(None, "fsdp")),
        check_vma=False,
    )
```

time: 1040 us -> 211 us (0.20)
  blocking collectives: 691 us -> 38.4 us
  waiting for transfers between devices: 130 us -> 43.7 us
  matrix products: 79.1 us -> 0 us
  Pallas kernels: 0 us -> 54 us
  other arithmetic: 48.9 us -> 11.8 us
  local copies, waits for them, and re-layouts: 24.5 us -> 6.99 us
  between operations: 15 us -> 3.19 us
    psum x1 -> x0, blocking collectives: 689 us -> none  [on_device(): summed = lax.psum(partial_value, ('span', 'sp'))]
    dot_general x21 -> x0, matrix products: 79.1 us -> none  [the longest x6 44.7 us: across(): lax.dot_general(left, right, (((1,), (1,)), ((), ())), preferred_element_...]
    pallas_call x0 -> x7, Pallas kernels: none -> 54 us  [the longest x3 37.6 us: unit(): pl.pallas_call(unit_kernel, grid=(GROUP // QTILE,), in_specs=[pl.BlockSpe...]
    unnamed x2 -> x0, waiting for transfers between devices: 37.5 us -> none
    all_to_all x0 -> x2, blocking collectives: none -> 35.3 us  [the longest x1 20 us: on_device(): own_b = to_sp(send_b)]
    all_to_all x7 -> x3, waiting for transfers between devices: 52 us -> 17.6 us  [the longest x1 17.6 us: on_device(): home_a = to_plane(out_a)]
    convert_element_type x9 -> x0, other arithmetic: 28.2 us -> none  [the longest x2 17.5 us: head_grads(): weights = (factor * probs).astype(jnp.bfloat16)]
    ppermute x4 -> x10, starting transfers between devices: 11.9 us -> 36.8 us  [the longest x4 15.2 us: shifted(): lax.ppermute(value, 'span', [(source, source + steps) for source in range...]
  transfers between devices with their start and end apart: 12 -> 13, of which waited for: 9 -> 7; matrix products, arithmetic and copies ran while one was open for 7% -> 8% of each run, Pallas kernels for 0% -> 21%
where the time goes in v1:
time: 211 us; the launch traced here: 208 us
  Pallas kernels  54 us (26%)
  starting transfers between devices  49.7 us (24%)
  waiting for transfers between devices  43.7 us (21%)
  blocking collectives  38.4 us (18%)
  other arithmetic  11.8 us (6%)
  local copies, waits for them, and re-layouts  6.99 us (3%)
  between operations  3.19 us (2%)
    pallas_call x3, Pallas kernels, unit(): pl.pallas_call(unit_kernel, grid=(GROUP // QTILE,), in_specs=[pl.BlockSpe...  37.6 us
    all_to_all x1, blocking collectives, on_device(): own_b = to_sp(send_b)  20 us
    ppermute x1, waiting for transfers between devices, on_device(): lax.ppermute(jnp.full((8, 128), bound, F32), 'span', [(i, i ^ 1) for i in...  18.6 us
    all_to_all x1, waiting for transfers between devices, on_device(): home_a = to_plane(out_a)  17.6 us
    all_to_all x1, blocking collectives, on_device(): shares = to_plane(jnp.broadcast_to(share[None], (heads_a, 8, HDIM)))  15.3 us
    ppermute x4, starting transfers between devices, shifted(): lax.ppermute(value, 'span', [(source, source + steps) for source in range...  15.2 us
    ppermute x3, starting transfers between devices, on_device(): lax.ppermute(share, 'span', [(i, i ^ reach) for i in range(n_span)])  13.9 us
    pallas_call x2, Pallas kernels, combine(): pl.pallas_call(functools.partial(combine_kernel, groups), grid=(1,), in_s...  6.58 us
  transfers between devices with their start and end apart: 13, of which 7 were waited for; matrix products, arithmetic and copies ran while one was open for 8% of the time, Pallas kernels for 21%

profile of v1, /device:TPU:0, one launch (start us, length us, event | category | flops | bytes accessed | tf_op | source)
XLA Modules:
  0.0 207.8 jit_solution(16256693913844353907)
XLA Ops:
  0.6 3.1 %all_gather.3.gain_ref = f32[2,3072]{1,0:T(2,128)} all-gather(f32[2,1536]{1,0:T(2,128)} %param.11), channel_id=1, replica_groups=mesh['span'=16,'sp'=8,'fsdp'=2] {'fsdp'}, dimensions={1}, use_global_device_ids=true | all-gather | bytes 36864 | tf_op jit(solution)/shard_map/all_gather | solution.py:301
  3.8 4.9 %pack.1 = (bf16[16,4,128,128]{3,2,1,0:T(8,128)(2,1)}, bf16[8,4,128,128]{3,2,1,0:T(8,128)(2,1)}) custom-call(bf16[128,3072]{1,0:T(8,128)(2,1)} %bitcast.27, bf16[128,3072]{1,0:T(8,128)(2,1)} %bitcast.29, bf16[128,3072]{1,0:T(8,128)(2,1)} %bitcast.31, bf16[128,3072]{1,0:T(8,128)(2,1)} %bitcast.32, f32[2,3072]{1,0:T(2,128)} %all_gather.3.gain_ref), custom_call_target="tpu_custom_call" | custom-call | flops 3932160 | bytes 6291456 | tf_op jit(solution)/shard_map/pack/pallas_call | solution.py:56
  8.6 20.0 %all_to_all.25.q_ref.g_ref.ko_ref.vo_ref.own_ref = bf16[8,4,128,128]{3,2,1,0:T(8,128)(2,1)S(1)} all-to-all(bf16[8,4,128,128]{3,2,1,0:T(8,128)(2,1)} %get-tuple-element.40), channel_id=1, replica_groups=mesh['span'=16,'sp'=8,'fsdp'=2] {'sp'}, dimensions={0} | all-to-all | bytes 2097152 | tf_op jit(solution)/shard_map/all_to_all | solution.py:303
  28.6 4.7 %all-to-all-start = ((bf16[16,4,128,128]{3,2,1,0:T(8,128)(2,1)}), bf16[16,4,128,128]{3,2,1,0:T(8,128)(2,1)S(1)}, u32[]{:S(2)}, u32[]{:S(2)}) async-start(bf16[16,4,128,128]{3,2,1,0:T(8,128)(2,1)} %get-tuple-element.28), calls=%async_computation | async-start | bytes 4194304 | tf_op jit(solution)/shard_map/all_to_all | solution.py:304
  33.3 0.5 slice.88
  33.8 1.3 fusion.3
  35.7 3.5 %collective-permute-start = (f32[8,128]{1,0:T(8,128)S(1)}, f32[8,128]{1,0:T(8,128)S(1)}, u32[]{:S(2)}, u32[]{:S(2)}) collective-permute-start(f32[8,128]{1,0:T(8,128)S(1)} %broadcast_in_dim.21), channel_id=1, source_target_pairs={{0,16},{16,0},{32,48},{48,32},{64,80},{80,64},{96,112},{112,96},{1... | collective-permute-start | bytes 12296 | tf_op jit(solution)/shard_map/ppermute | solution.py:308
  39.2 0.8 slice.120
  40.0 2.0 collective-permute-start.3
  42.1 0.1 constant_dynamic-slice_fusion
  42.2 0.6 fusion.11
  42.8 0.6 fusion.9
  43.4 2.4 %pad_add_fusion.2.info_ref = s32[4]{0:T(128)} fusion(s32[1]{0:T(128)} %bitcast.17, s32[1]{0:T(128)} %bitcast.16, s32[1]{0:T(128)} %bitcast.15, s32[1]{0:T(128)} %bitcast.14), kind=kLoop, calls=%fused_computation.20 | loop fusion | flops 12 | bytes 32 | tf_op jit(solution)/shard_map/stack | solution.py:318
  45.8 18.6 %collective-permute-done = f32[8,128]{1,0:T(8,128)S(1)} collective-permute-done((f32[8,128]{1,0:T(8,128)S(1)}, f32[8,128]{1,0:T(8,128)S(1)}, u32[]{:S(2)}, u32[]{:S(2)}) %collective-permute-start) | collective-permute-done | bytes 4128 | tf_op jit(solution)/shard_map/ppermute | solution.py:308
  64.4 0.5 slice.89
  66.2 10.6 %collective-permute-start.1 = (bf16[8,2,128,128]{3,2,1,0:T(8,128)(2,1)S(1)}, bf16[8,2,128,128]{3,2,1,0:T(8,128)(2,1)}, u32[]{:S(2)}, u32[]{:S(2)}) collective-permute-start(bf16[8,2,128,128]{3,2,1,0:T(8,128)(2,1)S(1)} %slice.117), channel_id=1, source_target_pairs={{0,32},{16,48},{32,64},{48,80},{64,96},{80,112},{96,128},{112,144}... | collective-permute-start | bytes 1572872 | tf_op jit(solution)/shard_map/ppermute | solution.py:287
  76.8 1.9 pad_add_fusion.info_ref
  79.3 0.8 copy-done.8
  80.1 12.5 %unit_b.1 = (bf16[1024,128]{1,0:T(8,128)(2,1)}, f32[1024,128]{1,0:T(8,128)}, f32[1024,128]{1,0:T(8,128)}, bf16[1024,128]{1,0:T(8,128)(2,1)}, bf16[1024,128]{1,0:T(8,128)(2,1)}) custom-call(s32[4]{0:T(128)} %pad_add_fusion.2.info_ref, bf16[8,4,128,128]{3,2,1,0:T(8,128)(2,1)} %copy-done.1, bf16[8,4,128,128]{3,2,1,0:T(8,128)(2,1)} %copy-done.1, ...), custom_call_target="tpu_custom_call" | custom-call | flops 2684354560 | bytes 3145728 | tf_op jit(solution)/shard_map/unit_b/pallas_call | solution.py:166
  92.6 1.1 pad_maximum_fusion.1
  93.7 1.3 collective-permute-start.4
  95.0 12.5 %unit_e.1 = (bf16[1024,128]{1,0:T(8,128)(2,1)}, f32[1024,128]{1,0:T(8,128)}, f32[1024,128]{1,0:T(8,128)}, bf16[1024,128]{1,0:T(8,128)(2,1)}, bf16[1024,128]{1,0:T(8,128)(2,1)}) custom-call(s32[4]{0:T(128)} %pad_add_fusion.info_ref, bf16[16,4,128,128]{3,2,1,0:T(8,128)(2,1)} %copy-done, bf16[16,4,128,128]{3,2,1,0:T(8,128)(2,1)} %copy-done, ...), custom_call_target="tpu_custom_call" | custom-call | flops 2684354560 | bytes 3145728 | tf_op jit(solution)/shard_map/unit_e/pallas_call | solution.py:166
  107.5 1.1 pad_maximum_fusion
  108.6 1.3 collective-permute-start.2
  109.9 2.0 pad_add_fusion.1.info_ref
  111.9 0.8 fusion.5
  112.7 2.7 %combine_b.1 = (bf16[8,3,128,128]{3,2,1,0:T(8,128)(2,1)}, f32[2,128]{1,0:T(2,128)}) custom-call(bf16[8,4,128,128]{3,2,1,0:T(8,128)(2,1)} %copy-done.1, bf16[1024,128]{1,0:T(8,128)(2,1)} %get-tuple-element.41.refs_0_, f32[1024,128]{1,0:T(8,128)} %get-tuple-element.42.refs_1_, f32[1024,128]{1,0:T(8,128)} %get-tuple-element.43.refs_2_, ...), custom_call_target="tpu_custom_call" | custom-call | flops 1310720 | bytes 2621440 | tf_op jit(solution)/shard_map/combine_b/pallas_call | solution.py:225
  115.4 4.5 %all-to-all-start.3 = ((bf16[8,3,128,128]{3,2,1,0:T(8,128)(2,1)}), bf16[8,3,128,128]{3,2,1,0:T(8,128)(2,1)S(1)}, u32[]{:S(2)}, u32[]{:S(2)}) async-start(bf16[8,3,128,128]{3,2,1,0:T(8,128)(2,1)} %get-tuple-element.46), calls=%async_computation.3 | async-start | bytes 1572864 | tf_op jit(solution)/shard_map/all_to_all | solution.py:326
  120.0 12.5 %unit_o.1 = (bf16[1024,128]{1,0:T(8,128)(2,1)}, f32[1024,128]{1,0:T(8,128)}, f32[1024,128]{1,0:T(8,128)}, bf16[1024,128]{1,0:T(8,128)(2,1)}, bf16[1024,128]{1,0:T(8,128)(2,1)}) custom-call(s32[4]{0:T(128)} %pad_add_fusion.1.info_ref, bf16[16,4,128,128]{3,2,1,0:T(8,128)(2,1)} %copy-done, bf16[16,4,128,128]{3,2,1,0:T(8,128)(2,1)} %copy-done, ...), custom_call_target="tpu_custom_call" | custom-call | flops 2684354560 | bytes 3145728 | tf_op jit(solution)/shard_map/unit_o/pallas_call | solution.py:166
  132.5 0.8 fusion.6
  133.4 3.9 %combine_a.1 = (bf16[16,3,128,128]{3,2,1,0:T(8,128)(2,1)}, f32[2,128]{1,0:T(2,128)}) custom-call(bf16[16,4,128,128]{3,2,1,0:T(8,128)(2,1)} %copy-done, bf16[1024,128]{1,0:T(8,128)(2,1)} %get-tuple-element.29.refs_0_, f32[1024,128]{1,0:T(8,128)} %get-tuple-element.30.refs_1_, f32[1024,128]{1,0:T(8,128)} %get-tuple-element.31.refs_2_, ...), custom_call_target="tpu_custom_call" | custom-call | flops 2621440 | bytes 5242880 | tf_op jit(solution)/shard_map/combine_a/pallas_call | solution.py:225
  137.3 0.8 maximum_maximum_fusion
  138.0 1.2 collective-permute-done.5
  139.2 0.7 fusion.4
  140.0 2.8 %collective-permute-start.6 = (f32[8,128]{1,0:T(8,128)S(1)}, f32[8,128]{1,0:T(8,128)S(1)}, u32[]{:S(2)}, u32[]{:S(2)}) collective-permute-start(f32[8,128]{1,0:T(8,128)S(1)} %fusion.4), channel_id=1, source_target_pairs={{0,32},{16,48},{32,0},{48,16},{64,96},{80,112},{96,64},{112,80},{1... | collective-permute-start | bytes 12296 | tf_op jit(solution)/shard_map/ppermute | solution.py:343
  142.7 1.6 collective-permute-done.6
  144.3 4.1 %collective-permute-start.7 = (f32[8,128]{1,0:T(8,128)S(1)}, f32[8,128]{1,0:T(8,128)S(1)}, u32[]{:S(2)}, u32[]{:S(2)}) collective-permute-start(f32[8,128]{1,0:T(8,128)S(1)} %add.37), channel_id=1, source_target_pairs={{0,64},{16,80},{32,96},{48,112},{64,0},{80,16},{96,32},{112,48},{1... | collective-permute-start | bytes 12296 | tf_op jit(solution)/shard_map/ppermute | solution.py:343
  148.4 1.6 collective-permute-done.7
  150.0 7.1 %collective-permute-start.8 = (f32[8,128]{1,0:T(8,128)S(1)}, f32[8,128]{1,0:T(8,128)S(1)}, u32[]{:S(2)}, u32[]{:S(2)}) collective-permute-start(f32[8,128]{1,0:T(8,128)S(1)} %add.38), channel_id=1, source_target_pairs={{0,128},{16,144},{32,160},{48,176},{64,192},{80,208},{96,224},{112... | collective-permute-start | bytes 12296 | tf_op jit(solution)/shard_map/ppermute | solution.py:343
  157.0 1.6 collective-permute-done.8
  158.6 4.1 %collective-permute-start.9 = (f32[8,128]{1,0:T(8,128)S(1)}, f32[8,128]{1,0:T(8,128)S(1)}, u32[]{:S(2)}, u32[]{:S(2)}) collective-permute-start(f32[8,128]{1,0:T(8,128)S(1)} %add.39), channel_id=1, source_target_pairs={{0,16},{16,0},{32,48},{48,32},{64,80},{80,64},{96,112},{112,96},{1... | collective-permute-start | bytes 12296 | tf_op jit(solution)/shard_map/ppermute | solution.py:345
  162.7 1.6 collective-permute-done.9
  164.4 15.3 %all_to_all.26 = f32[16,8,128]{2,1,0:T(8,128)S(1)} all-to-all(f32[16,8,128]{2,1,0:T(8,128)S(1)} %broadcast_in_dim.26), channel_id=1, replica_groups={{0,2,4,6,8,10,12,14,16,18,20,22,24,26,28,30},{32,34,36,38,40,42,44,46,4..., dimensions={0} | all-to-all | bytes 131072 | tf_op jit(solution)/shard_map/all_to_all | solution.py:347
  179.7 3.7 %all-to-all-start.1 = ((bf16[16,3,128,128]{3,2,1,0:T(8,128)(2,1)}), bf16[16,3,128,128]{3,2,1,0:T(8,128)(2,1)S(1)}, u32[]{:S(2)}, u32[]{:S(2)}) async-start(bf16[16,3,128,128]{3,2,1,0:T(8,128)(2,1)} %get-tuple-element.39), calls=%async_computation.1 | async-start | bytes 3145728 | tf_op jit(solution)/shard_map/all_to_all | solution.py:337
  183.5 0.6 fusion.2
  184.1 17.6 %all-to-all-done.1.a_ref = bf16[16,3,128,128]{3,2,1,0:T(8,128)(2,1)S(1)} async-done(((bf16[16,3,128,128]{3,2,1,0:T(8,128)(2,1)}), bf16[16,3,128,128]{3,2,1,0:T(8,128)(2,1)S(1)}, u32[]{:S(2)}, u32[]{:S(2)}) %all-to-all-start.1) | async-done | bytes 1572896 | tf_op jit(solution)/shard_map/all_to_all | solution.py:337
  201.7 1.2 copy-done.2
  202.9 4.9 %finish.1 = (bf16[128,3072]{1,0:T(8,128)(2,1)}, bf16[128,3072]{1,0:T(8,128)(2,1)}, bf16[128,3072]{1,0:T(8,128)(2,1)}) custom-call(bf16[128,3072]{1,0:T(8,128)(2,1)} %bitcast.28, bf16[128,3072]{1,0:T(8,128)(2,1)} %bitcast.30, f32[2,3072]{1,0:T(2,128)} %all_gather.3.gain_ref, bf16[16,3,128,128]{3,2,1,0:T(8,128)(2,1)} %copy-done.2, ...), custom_call_target="tpu_custom_call" | custom-call | flops 11796480 | bytes 6291456 | tf_op jit(solution)/shard_map/finish/pallas_call | solution.py:267
  (38 shorter events, 0.2 us)
Async XLA Ops:
  28.6 10.6 %copy-start.1 = (bf16[8,4,128,128]{3,2,1,0:T(8,128)(2,1)}, bf16[8,4,128,128]{3,2,1,0:T(8,128)(2,1)S(1)}, u32[]{:S(2)}) copy-start(bf16[8,4,128,128]{3,2,1,0:T(8,128)(2,1)S(1)} %all_to_all.25.q_ref.g_ref.ko_ref.vo_ref.own_ref) | copy-start | bytes 3145732
  28.6 4.7 %copy-start.6 = (s32[1,1024]{1,0:T(1,128)S(1)}, s32[1,1024]{1,0:T(1,128)}, u32[]{:S(2)}) copy-start(s32[1,1024]{1,0:T(1,128)} %param.12) | copy-start | bytes 12292
  28.6 13.5 %copy-start.5 = (s32[1,32]{1,0:T(1,128)S(1)}, s32[1,32]{1,0:T(1,128)}, u32[]{:S(2)}) copy-start(s32[1,32]{1,0:T(1,128)} %param.13) | copy-start | bytes 388
  28.6 37.6 %all-to-all-start = ((bf16[16,4,128,128]{3,2,1,0:T(8,128)(2,1)}), bf16[16,4,128,128]{3,2,1,0:T(8,128)(2,1)S(1)}, u32[]{:S(2)}, u32[]{:S(2)}) async-start(bf16[16,4,128,128]{3,2,1,0:T(8,128)(2,1)} %get-tuple-element.28), calls=%async_computation | async-start | bytes 4194304 | tf_op jit(solution)/shard_map/all_to_all | solution.py:304
  35.7 28.7 %collective-permute-start = (f32[8,128]{1,0:T(8,128)S(1)}, f32[8,128]{1,0:T(8,128)S(1)}, u32[]{:S(2)}, u32[]{:S(2)}) collective-permute-start(f32[8,128]{1,0:T(8,128)S(1)} %broadcast_in_dim.21), channel_id=1, source_target_pairs={{0,16},{16,0},{32,48},{48,32},{64,80},{80,64},{96,112},{112,96},{1... | collective-permute-start | bytes 12296 | tf_op jit(solution)/shard_map/ppermute | solution.py:308
  40.0 39.2 %collective-permute-start.3 = (bf16[8,2,128,128]{3,2,1,0:T(8,128)(2,1)}, bf16[8,2,128,128]{3,2,1,0:T(8,128)(2,1)S(1)}, u32[]{:S(2)}, u32[]{:S(2)}) collective-permute-start(bf16[8,2,128,128]{3,2,1,0:T(8,128)(2,1)} %slice.120), channel_id=1, source_target_pairs={{0,16},{16,32},{32,48},{48,64},{64,80},{80,96},{96,112},{112,128},... | collective-permute-start | bytes 1572872 | tf_op jit(solution)/shard_map/ppermute | solution.py:287
  66.2 26.5 %copy-start = (bf16[16,4,128,128]{3,2,1,0:T(8,128)(2,1)}, bf16[16,4,128,128]{3,2,1,0:T(8,128)(2,1)S(1)}, u32[]{:S(2)}) copy-start(bf16[16,4,128,128]{3,2,1,0:T(8,128)(2,1)S(1)} %all-to-all-done.q_ref.g_ref.ko_ref.vo_ref.kp_ref.vp_ref.own_ref) | copy-start | bytes 6291460
  66.2 28.8 %collective-permute-start.1 = (bf16[8,2,128,128]{3,2,1,0:T(8,128)(2,1)S(1)}, bf16[8,2,128,128]{3,2,1,0:T(8,128)(2,1)}, u32[]{:S(2)}, u32[]{:S(2)}) collective-permute-start(bf16[8,2,128,128]{3,2,1,0:T(8,128)(2,1)S(1)} %slice.117), channel_id=1, source_target_pairs={{0,32},{16,48},{32,64},{48,80},{64,96},{80,112},{96,128},{112,144}... | collective-permute-start | bytes 1572872 | tf_op jit(solution)/shard_map/ppermute | solution.py:287
  79.3 0.8 copy-start.8
  93.7 18.2 %collective-permute-start.4 = (bf16[2048,128]{1,0:T(8,128)(2,1)S(1)}, bf16[2048,128]{1,0:T(8,128)(2,1)S(1)}, u32[]{:S(2)}, u32[]{:S(2)}) collective-permute-start(bf16[2048,128]{1,0:T(8,128)(2,1)S(1)} %pad_maximum_fusion.1), channel_id=1, source_target_pairs={{16,0},{32,16},{48,32},{64,48},{80,64},{96,80},{112,96},{128,112},... | collective-permute-start | bytes 1572872 | tf_op jit(solution)/shard_map/ppermute | solution.py:287
  108.6 23.9 %collective-permute-start.2 = (bf16[2048,128]{1,0:T(8,128)(2,1)S(1)}, bf16[2048,128]{1,0:T(8,128)(2,1)S(1)}, u32[]{:S(2)}, u32[]{:S(2)}) collective-permute-start(bf16[2048,128]{1,0:T(8,128)(2,1)S(1)} %pad_maximum_fusion), channel_id=1, source_target_pairs={{32,0},{48,16},{64,32},{80,48},{96,64},{112,80},{128,96},{144,112}... | collective-permute-start | bytes 1572872 | tf_op jit(solution)/shard_map/ppermute | solution.py:287
  115.4 48.9 %all-to-all-start.3 = ((bf16[8,3,128,128]{3,2,1,0:T(8,128)(2,1)}), bf16[8,3,128,128]{3,2,1,0:T(8,128)(2,1)S(1)}, u32[]{:S(2)}, u32[]{:S(2)}) async-start(bf16[8,3,128,128]{3,2,1,0:T(8,128)(2,1)} %get-tuple-element.46), calls=%async_computation.3 | async-start | bytes 1572864 | tf_op jit(solution)/shard_map/all_to_all | solution.py:326
  133.4 3.9 %copy-start.7 = (f32[2,128]{1,0:T(2,128)S(1)}, f32[2,128]{1,0:T(2,128)}, u32[]{:S(2)}) copy-start(f32[2,128]{1,0:T(2,128)} %get-tuple-element.51) | copy-start | bytes 3076
  137.3 46.2 %copy-start.4 = (f32[2,1536]{1,0:T(2,128)S(1)}, f32[2,1536]{1,0:T(2,128)}, u32[]{:S(2)}) copy-start(f32[2,1536]{1,0:T(2,128)} %param.11) | copy-start | bytes 36868
  138.0 1.2 collective-permute-start.5
  140.0 4.4 %collective-permute-start.6 = (f32[8,128]{1,0:T(8,128)S(1)}, f32[8,128]{1,0:T(8,128)S(1)}, u32[]{:S(2)}, u32[]{:S(2)}) collective-permute-start(f32[8,128]{1,0:T(8,128)S(1)} %fusion.4), channel_id=1, source_target_pairs={{0,32},{16,48},{32,0},{48,16},{64,96},{80,112},{96,64},{112,80},{1... | collective-permute-start | bytes 12296 | tf_op jit(solution)/shard_map/ppermute | solution.py:343
  144.3 5.7 %collective-permute-start.7 = (f32[8,128]{1,0:T(8,128)S(1)}, f32[8,128]{1,0:T(8,128)S(1)}, u32[]{:S(2)}, u32[]{:S(2)}) collective-permute-start(f32[8,128]{1,0:T(8,128)S(1)} %add.37), channel_id=1, source_target_pairs={{0,64},{16,80},{32,96},{48,112},{64,0},{80,16},{96,32},{112,48},{1... | collective-permute-start | bytes 12296 | tf_op jit(solution)/shard_map/ppermute | solution.py:343
  150.0 8.6 %collective-permute-start.8 = (f32[8,128]{1,0:T(8,128)S(1)}, f32[8,128]{1,0:T(8,128)S(1)}, u32[]{:S(2)}, u32[]{:S(2)}) collective-permute-start(f32[8,128]{1,0:T(8,128)S(1)} %add.38), channel_id=1, source_target_pairs={{0,128},{16,144},{32,160},{48,176},{64,192},{80,208},{96,224},{112... | collective-permute-start | bytes 12296 | tf_op jit(solution)/shard_map/ppermute | solution.py:343
  158.6 5.7 %collective-permute-start.9 = (f32[8,128]{1,0:T(8,128)S(1)}, f32[8,128]{1,0:T(8,128)S(1)}, u32[]{:S(2)}, u32[]{:S(2)}) collective-permute-start(f32[8,128]{1,0:T(8,128)S(1)} %add.39), channel_id=1, source_target_pairs={{0,16},{16,0},{32,48},{48,32},{64,80},{80,64},{96,112},{112,96},{1... | collective-permute-start | bytes 12296 | tf_op jit(solution)/shard_map/ppermute | solution.py:345
  164.4 37.4 %copy-start.3 = (bf16[8,3,128,128]{3,2,1,0:T(8,128)(2,1)}, bf16[8,3,128,128]{3,2,1,0:T(8,128)(2,1)S(1)}, u32[]{:S(2)}) copy-start(bf16[8,3,128,128]{3,2,1,0:T(8,128)(2,1)S(1)} %all-to-all-done.3.b_ref) | copy-start | bytes 2359300
  179.7 22.0 %all-to-all-start.1 = ((bf16[16,3,128,128]{3,2,1,0:T(8,128)(2,1)}), bf16[16,3,128,128]{3,2,1,0:T(8,128)(2,1)S(1)}, u32[]{:S(2)}, u32[]{:S(2)}) async-start(bf16[16,3,128,128]{3,2,1,0:T(8,128)(2,1)} %get-tuple-element.39), calls=%async_computation.1 | async-start | bytes 3145728 | tf_op jit(solution)/shard_map/all_to_all | solution.py:337
  201.7 1.2 copy-start.2

commit v2 on v1

v2 whole, which is shorter than its diff:
```python
import functools

import jax
import jax.numpy as jnp
from jax import lax
from jax.experimental import pallas as pl
from jax.experimental.pallas import tpu as pltpu
from jax.sharding import PartitionSpec as P


HDIM = 128
TOK = 128
GROUP = 1024
KCHUNK = 512
EPSILON = 1e-06
NEGATIVE = -1e30
LOG2E = 1.4426950408889634
SCALE = HDIM ** (-0.5)
F32 = jnp.float32
BF16 = jnp.bfloat16


def nt(left, right):
    return lax.dot_general(left, right, (((1,), (1,)), ((), ())), preferred_element_type=F32)


def nn(left, right):
    return lax.dot_general(left, right, (((1,), (0,)), ((), ())), preferred_element_type=F32)


def pack_kernel(heads_a, q_ref, k_ref, v_ref, g_ref, gain_ref, kv_ref, qg_ref, b_ref):
    heads = q_ref.shape[1] // HDIM

    def put(ref, slot_a, slot_b, rows):
        for head in range(heads):
            piece = rows[:, head * HDIM : (head + 1) * HDIM]
            if head < heads_a:
                ref[head, slot_a] = piece
            else:
                b_ref[head - heads_a, slot_b] = piece

    def normed(ref, row):
        wide = ref[...].astype(F32)
        inverse = lax.rsqrt(jnp.mean(wide * wide, axis=1, keepdims=True) + EPSILON)
        return (wide * inverse * gain_ref[row : row + 1, :]).astype(BF16)

    put(kv_ref, 0, 0, normed(k_ref, 1))
    put(kv_ref, 1, 1, v_ref[...])
    put(qg_ref, 0, 2, normed(q_ref, 0))
    put(qg_ref, 1, 3, g_ref[...])


def pack(query_pre, key_pre, values, cotangent, gain_full, heads_a):
    tokens, channels = query_pre.shape
    heads_b = channels // HDIM - heads_a
    step = 32
    rows = pl.BlockSpec((step, channels), lambda i: (i, 0))

    def slabs(heads, slots):
        return pl.BlockSpec((heads, slots, step, HDIM), lambda i: (0, 0, i, 0))

    return pl.pallas_call(
        functools.partial(pack_kernel, heads_a),
        grid=(tokens // step,),
        in_specs=[rows] * 4 + [pl.BlockSpec((2, channels), lambda i: (0, 0))],
        out_specs=[slabs(heads_a, 2), slabs(heads_a, 2), slabs(heads_b, 4)],
        out_shape=[
            jax.ShapeDtypeStruct((heads_a, 2, tokens, HDIM), BF16),
            jax.ShapeDtypeStruct((heads_a, 2, tokens, HDIM), BF16),
            jax.ShapeDtypeStruct((heads_b, 4, tokens, HDIM), BF16),
        ],
        name="pack",
        cost_estimate=pl.CostEstimate(
            flops=10 * tokens * channels, bytes_accessed=16 * tokens * channels, transcendentals=tokens
        ),
    )(query_pre, key_pre, values, cotangent, gain_full)


def unit_kernel(
    line, info_ref, q_ref, g_ref, ko_ref, vo_ref, kp_ref, vp_ref,
    dq_ref, dko_ref, dvo_ref, back_ref, gain_ref,
    p_ref, dp_ref,
):
    chunks = 2 * GROUP // KCHUNK
    own_chunks = GROUP // KCHUNK

    def part_of(own_ref, prev_ref, chunk):
        ref = own_ref if chunk < own_chunks else prev_ref
        first = chunk % own_chunks * KCHUNK // TOK
        return ref[first : first + KCHUNK // TOK].reshape(KCHUNK, HDIM)

    keys_at = functools.partial(part_of, ko_ref, kp_ref)
    values_at = functools.partial(part_of, vo_ref, vp_ref)
    bound = info_ref[line, 0]
    is_open = info_ref[line, 1] > 0
    early_weight = info_ref[line, 2].astype(F32)
    late_weight = info_ref[line, 3].astype(F32)
    q = q_ref[...].reshape(GROUP, HDIM)
    g = g_ref[...].reshape(GROUP, HDIM)
    early = lax.broadcasted_iota(jnp.int32, (1, GROUP), 1) < bound
    reach = jnp.where(early, bound, GROUP)
    weight = jnp.where(early, early_weight, late_weight)
    factor = SCALE * LOG2E

    pieces = []
    for chunk in range(chunks):
        span = slice(chunk * KCHUNK, (chunk + 1) * KCHUNK)
        scores = nt(keys_at(chunk), q)
        if chunk < own_chunks and (chunk + 1) * KCHUNK > GROUP // 4:
            row = chunk * KCHUNK + lax.broadcasted_iota(jnp.int32, (KCHUNK, GROUP), 0)
            scores = jnp.where(row < reach, scores, NEGATIVE)
        top = jnp.max(scores, axis=0, keepdims=True) * factor
        probs = jnp.exp2(scores * factor - top)
        grads = nt(values_at(chunk), g)
        p_ref[span] = probs
        dp_ref[span] = grads
        if chunk >= own_chunks:
            top = jnp.where(is_open, top, NEGATIVE)
        pieces.append((top, jnp.sum(probs, axis=0, keepdims=True), jnp.sum(probs * grads, axis=0, keepdims=True)))
    row_max = functools.reduce(jnp.maximum, [piece[0] for piece in pieces])
    lifts = [jnp.exp2(piece[0] - row_max) for piece in pieces]
    total = sum(lift * piece[1] for lift, piece in zip(lifts, pieces))
    inner = sum(lift * piece[2] for lift, piece in zip(lifts, pieces))
    over = 1.0 / total
    delta = inner * over
    dq_t = jnp.zeros((HDIM, GROUP), F32)
    for chunk in range(chunks):
        span = slice(chunk * KCHUNK, (chunk + 1) * KCHUNK)
        weights = p_ref[span] * (weight * over * lifts[chunk])
        sgrad = (weights * (dp_ref[span] - delta)).astype(BF16)
        dk = nn(sgrad, q) * SCALE
        dv = nn(weights.astype(BF16), g)
        if chunk < own_chunks:
            dko_ref[span] = dk
            dvo_ref[span] = dv
        else:
            back_ref[chunk * KCHUNK - GROUP : (chunk + 1) * KCHUNK - GROUP] = dk.astype(BF16)
            back_ref[chunk * KCHUNK : (chunk + 1) * KCHUNK] = dv.astype(BF16)
        dq_t = dq_t + nn(keys_at(chunk).T, sgrad)
    dq = (dq_t * SCALE).T
    gain_ref[...] = jnp.broadcast_to(jnp.sum(dq * q.astype(F32), axis=0, keepdims=True), (8, HDIM))
    dq_ref[...] = dq.astype(BF16)


def unit(line, info, queries, own, prev):
    slabs = GROUP // TOK

    def whole(source, which):
        _, at, slots = source
        return pl.BlockSpec((slabs, None, TOK, HDIM), lambda i: (at, slots[which], 0, 0))

    full = pl.BlockSpec((GROUP, HDIM), lambda i: (0, 0))
    return pl.pallas_call(
        functools.partial(unit_kernel, line),
        grid=(1,),
        in_specs=[pl.BlockSpec(memory_space=pltpu.SMEM)]
        + [whole(source, which) for source in (queries, own, prev) for which in (0, 1)],
        out_specs=[
            full, full, full,
            pl.BlockSpec((2 * GROUP, HDIM), lambda i: (0, 0)),
            pl.BlockSpec((8, HDIM), lambda i: (0, 0)),
        ],
        out_shape=[
            jax.ShapeDtypeStruct((GROUP, HDIM), BF16),
            jax.ShapeDtypeStruct((GROUP, HDIM), F32),
            jax.ShapeDtypeStruct((GROUP, HDIM), F32),
            jax.ShapeDtypeStruct((2 * GROUP, HDIM), BF16),
            jax.ShapeDtypeStruct((8, HDIM), F32),
        ],
        scratch_shapes=[
            pltpu.VMEM((2 * GROUP, GROUP), F32),
            pltpu.VMEM((2 * GROUP, GROUP), F32),
        ],
        cost_estimate=pl.CostEstimate(
            flops=20 * GROUP * GROUP * HDIM, bytes_accessed=3 << 20, transcendentals=2 * GROUP * GROUP
        ),
    )(info, queries[0], queries[0], own[0], own[0], prev[0], prev[0])


def combine_kernel(groups, *refs):
    ins, out_ref = refs[: 4 * groups], refs[-1]
    slabs = out_ref.shape[0] // groups
    for group in range(groups):
        dq, dk, dv, back = ins[4 * group : 4 * group + 4]
        at = slice(group * slabs, (group + 1) * slabs)
        out_ref[at, :TOK] = dq[...].reshape(slabs, TOK, HDIM)
        out_ref[at, TOK : 2 * TOK] = (dk[...] + back[:GROUP].astype(F32)).astype(BF16).reshape(slabs, TOK, HDIM)
        out_ref[at, 2 * TOK : 3 * TOK] = (dv[...] + back[GROUP:].astype(F32)).astype(BF16).reshape(slabs, TOK, HDIM)


def combine(parts):
    groups = len(parts)
    slabs = groups * GROUP // TOK
    flat = [array for part in parts for array in part]
    full = pl.BlockSpec((GROUP, HDIM), lambda i: (0, 0))
    back = pl.BlockSpec((2 * GROUP, HDIM), lambda i: (0, 0))
    specs = [full, full, full, back] * groups
    depth = 3 * TOK
    return pl.pallas_call(
        functools.partial(combine_kernel, groups),
        grid=(1,),
        in_specs=specs,
        out_specs=pl.BlockSpec((slabs, depth, HDIM), lambda i: (0, 0, 0)),
        out_shape=jax.ShapeDtypeStruct((slabs, depth, HDIM), BF16),
        cost_estimate=pl.CostEstimate(
            flops=10 * groups * GROUP * HDIM, bytes_accessed=groups * GROUP * HDIM * 20, transcendentals=0
        ),
    )(*flat)


def finish_kernel(heads_a, heads_b, x_ref, y_ref, gain_ref, *refs):
    blocks, (qg_ref, kg_ref, vg_ref) = refs[:6], refs[6:]
    channels = x_ref.shape[1]

    def piece(head, slot):
        return blocks[slot][head] if head < heads_a else blocks[3 + slot][head - heads_a]

    for slot, ref, out in ((0, x_ref, qg_ref), (1, y_ref, kg_ref)):
        wide = ref[...].astype(F32)
        inverse = lax.rsqrt(jnp.mean(wide * wide, axis=1, keepdims=True) + EPSILON)
        normal = wide * inverse
        up = jnp.concatenate([piece(h, slot).astype(F32) for h in range(heads_a + heads_b)], axis=1)
        scaled = up * gain_ref[slot : slot + 1, :]
        inner = jnp.sum(scaled * normal, axis=1, keepdims=True) * (1.0 / channels)
        out[...] = (inverse * (scaled - normal * inner)).astype(BF16)
    for head in range(heads_a + heads_b):
        vg_ref[:, head * HDIM : (head + 1) * HDIM] = piece(head, 2)


def finish(query_pre, key_pre, gain_full, home_a, home_b):
    tokens, channels = query_pre.shape
    heads_a, heads_b = home_a.shape[0], home_b.shape[0]
    step = 32
    rows = pl.BlockSpec((step, channels), lambda i: (i, 0))

    def block(heads, slot):
        return pl.BlockSpec((heads, step, HDIM), lambda i: (0, slot * (tokens // step) + i, 0))

    return pl.pallas_call(
        functools.partial(finish_kernel, heads_a, heads_b),
        grid=(tokens // step,),
        in_specs=[rows, rows, pl.BlockSpec((2, channels), lambda i: (0, 0))]
        + [block(heads_a, slot) for slot in range(3)]
        + [block(heads_b, slot) for slot in range(3)],
        out_specs=[rows] * 3,
        out_shape=[jax.ShapeDtypeStruct((tokens, channels), BF16)] * 3,
        name="finish",
        cost_estimate=pl.CostEstimate(
            flops=30 * tokens * channels, bytes_accessed=16 * tokens * channels, transcendentals=tokens
        ),
    )(query_pre, key_pre, gain_full, home_a, home_a, home_a, home_b, home_b, home_b)


def shifted(value, steps, count):
    first, last = (max(0, -steps), min(count, count - steps))
    return lax.ppermute(value, "span", [(source, source + steps) for source in range(first, last)])


def swapped(value, axis, bit, count):
    return lax.ppermute(value, axis, [(i, i ^ bit) for i in range(count)])


def lines_of(bound, other, span, table):
    odd = span % 2
    even = span - odd
    row = lax.iota(jnp.int32, 3)
    groups = jnp.where(row == 0, span, even + row - 1)
    bounds = jnp.where((row == 0) | (groups == span), bound, other)
    spans = 2 * groups[:, None] + lax.iota(jnp.int32, 8)[None, :] - 2
    match = spans[:, :, None] == lax.iota(jnp.int32, table.shape[0])[None, None, :]
    weights = jnp.sum(jnp.where(match, table[None, None, :], 0), axis=2)
    column = lax.iota(jnp.int32, 8)[None, :]
    opens = (groups > 0).astype(jnp.int32)
    return jnp.where(column == 0, bounds[:, None], jnp.where(column == 1, opens[:, None], weights))


def on_device(query_pre, key_pre, values, cotangent, gains, frame_span, denoise_steps):
    n_span, n_sp = lax.axis_size("span"), lax.axis_size("sp")
    heads_a = 2 * n_sp
    slabs = GROUP // TOK
    plane = [[first + i for i in range(heads_a)] for first in range(0, n_span * n_sp, heads_a)]

    def to_plane(value):
        return lax.all_to_all(
            value, ("span", "sp"), split_axis=0, concat_axis=0, tiled=True, axis_index_groups=plane
        )

    def to_sp(value):
        return lax.all_to_all(value, "sp", split_axis=0, concat_axis=0, tiled=True)

    span = lax.axis_index("span")
    gain_full = lax.all_gather(gains, "fsdp", axis=1, tiled=True)
    send_kv, send_qg, send_b = pack(query_pre[0], key_pre[0], values[0], cotangent[0], gain_full, heads_a)
    own_b = to_sp(send_b)
    kv = to_plane(send_kv)
    qg = to_plane(send_qg)

    ids = frame_span[0]
    bound = jnp.sum((ids == ids[0]).astype(jnp.int32))
    other = swapped(jnp.full((8, HDIM), bound, F32), "span", 1, n_span)[0, 0].astype(jnp.int32)
    info = lines_of(bound, other, span, denoise_steps[0])

    prev_b = shifted(own_b[:, 0:2], 1, n_span)
    dq_b, dk_b, dv_b, term_b, gain_b = unit(0, info, (own_b, 0, (2, 3)), (own_b, 0, (0, 1)), (prev_b, 0, (0, 1)))
    back_b = shifted(term_b, -1, n_span)
    out_b = combine([(dq_b, dk_b, dv_b, back_b)])
    home_b = to_sp(out_b)

    prev_a = shifted(kv[slabs:], 2, n_span)
    dq_e, dk_e, dv_e, term_e, gain_e = unit(1, info, (qg, 0, (0, 1)), (kv, 0, (0, 1)), (prev_a, 0, (0, 1)))
    back_a = shifted(term_e, -2, n_span)
    dq_o, dk_o, dv_o, term_o, gain_o = unit(2, info, (qg, 1, (0, 1)), (kv, 1, (0, 1)), (kv, 0, (0, 1)))

    out_a = combine([(dq_e, dk_e, dv_e, term_o), (dq_o, dk_o, dv_o, back_a)])
    home_a = to_plane(out_a)

    share = jnp.concatenate([gain_e[0:1] + gain_o[0:1], gain_b[0:1], jnp.zeros((6, HDIM), F32)], axis=0)
    share = share + swapped(share, "fsdp", 1, 2)
    reach = 2
    while reach < n_span:
        share = share + swapped(share, "span", reach, n_span)
        reach *= 2
    lines = to_plane(jnp.broadcast_to(share[None], (heads_a, 8, HDIM)))
    table = jnp.concatenate([lines[:, 0], lines[:n_sp, 1] + lines[n_sp:, 1]], axis=0)
    half = heads_a + n_sp >> 1
    mine = jnp.where(lax.axis_index("fsdp") == 0, table[:half], table[half:]).reshape(1, half * HDIM)
    gain_grad = mine / gains

    query_back, key_back, value_back = finish(query_pre[0], key_pre[0], gain_full, home_a, home_b)
    return (query_back[None], key_back[None], value_back[None], gain_grad)


def solution(mesh):
    rows = P("fsdp", ("span", "sp"), None)
    return jax.shard_map(
        on_device,
        mesh=mesh,
        in_specs=(rows, rows, rows, rows, P(None, "fsdp"), P("fsdp", "span"), P("fsdp", None)),
        out_specs=(rows, rows, rows, P(None, "fsdp")),
        check_vma=False,
    )
```

time: 211 us -> 212 us (level)
  waiting for transfers between devices: 43.7 us -> 63.5 us
  blocking collectives: 38.4 us -> 23.1 us
  starting transfers between devices: 49.7 us -> 60.7 us
  Pallas kernels: 54 us -> 46 us
  other arithmetic: 11.8 us -> 4.45 us
    all_to_all x3 -> x5, waiting for transfers between devices: 17.6 us -> 36.8 us  [the longest x4 36.8 us: to_plane(): lax.all_to_all(value, ('span', 'sp'), split_axis=0, concat_axis=0, tiled=...]
    all_to_all x2 -> x1, blocking collectives: 35.3 us -> 20 us  [to_sp(): return lax.all_to_all(value, 'sp', split_axis=0, concat_axis=0, tiled=True)]
    ppermute x4, waiting for transfers between devices: 0.01 us -> 10.9 us  [shifted(): lax.ppermute(value, 'span', [(source, source + steps) for source in range...]
    ppermute x6 -> x5, waiting for transfers between devices: 26.1 us -> 15.7 us  [swapped(): return lax.ppermute(value, axis, [(i, i ^ bit) for i in range(count)])]
    all_to_all x3 -> x5, starting transfers between devices: 13 us -> 21.9 us  [the longest x4 18.4 us: to_plane(): lax.all_to_all(value, ('span', 'sp'), split_axis=0, concat_axis=0, tiled=...]
    pallas_call x3, Pallas kernels: 37.6 us -> 30.5 us  [unit(): pl.pallas_call(functools.partial(unit_kernel, line), grid=(1,), in_specs=...]
    another operation x3 -> x0, other arithmetic: 6.25 us -> none  [info_of(): jnp.stack([limit, (group > 0).astype(jnp.int32), weights[0], weights[1]])]
    ppermute x6 -> x5, starting transfers between devices: 21.5 us -> 27 us  [swapped(): return lax.ppermute(value, axis, [(i, i ^ bit) for i in range(count)])]
  transfers between devices with their start and end apart: 13 -> 14, of which waited for: 7 -> 8; matrix products, arithmetic and copies ran while one was open for 8% -> 3% of each run, Pallas kernels for 21% -> 13%
where the time goes in v2:
time: 212 us; the launch traced here: 209 us
  waiting for transfers between devices  63.5 us (30%)
  starting transfers between devices  60.7 us (29%)
  Pallas kernels  46 us (22%)
  blocking collectives  23.1 us (11%)
  local copies, waits for them, and re-layouts  8.8 us (4%)
  other arithmetic  4.45 us (2%)
  between operations  2.38 us (1%)
    all_to_all x4, waiting for transfers between devices, to_plane(): lax.all_to_all(value, ('span', 'sp'), split_axis=0, concat_axis=0, tiled=...  36.8 us
    pallas_call x3, Pallas kernels, unit(): pl.pallas_call(functools.partial(unit_kernel, line), grid=(1,), in_specs=...  30.5 us
    ppermute x5, starting transfers between devices, swapped(): return lax.ppermute(value, axis, [(i, i ^ bit) for i in range(count)])  27 us
    all_to_all x1, blocking collectives, to_sp(): return lax.all_to_all(value, 'sp', split_axis=0, concat_axis=0, tiled=True)  20 us
    all_to_all x4, starting transfers between devices, to_plane(): lax.all_to_all(value, ('span', 'sp'), split_axis=0, concat_axis=0, tiled=...  18.4 us
    ppermute x5, waiting for transfers between devices, swapped(): return lax.ppermute(value, axis, [(i, i ^ bit) for i in range(count)])  15.7 us
    ppermute x4, starting transfers between devices, shifted(): lax.ppermute(value, 'span', [(source, source + steps) for source in range...  11.8 us
    ppermute x4, waiting for transfers between devices, shifted(): lax.ppermute(value, 'span', [(source, source + steps) for source in range...  10.9 us
  transfers between devices with their start and end apart: 14, of which 8 were waited for; matrix products, arithmetic and copies ran while one was open for 3% of the time, Pallas kernels for 13%

profile of v2, /device:TPU:0, one launch (start us, length us, event | category | flops | bytes accessed | tf_op | source)
XLA Modules:
  0.0 208.9 jit_solution(4622228634948042093)
XLA Ops:
  0.6 3.1 %all_gather.3.gain_ref = f32[2,3072]{1,0:T(2,128)} all-gather(f32[2,1536]{1,0:T(2,128)} %param.11), channel_id=1, replica_groups=mesh['span'=16,'sp'=8,'fsdp'=2] {'fsdp'}, dimensions={1}, use_global_device_ids=true | all-gather | bytes 36864 | tf_op jit(solution)/shard_map/all_gather | solution.py:292
  3.8 4.8 %pack.1 = (bf16[16,2,128,128]{3,2,1,0:T(8,128)(2,1)}, bf16[16,2,128,128]{3,2,1,0:T(8,128)(2,1)}, bf16[8,4,128,128]{3,2,1,0:T(8,128)(2,1)}) custom-call(bf16[128,3072]{1,0:T(8,128)(2,1)} %bitcast.18, bf16[128,3072]{1,0:T(8,128)(2,1)} %bitcast.20, bf16[128,3072]{1,0:T(8,128)(2,1)} %bitcast.22, bf16[128,3072]{1,0:T(8,128)(2,1)} %bitcast.23, ...), custom_call_target="tpu_custom_call" | custom-call | flops 3932160 | bytes 6291456 | tf_op jit(solution)/shard_map/pack/pallas_call | solution.py:62
  8.5 20.0 %all_to_all.30.q_ref.g_ref.ko_ref.vo_ref = bf16[8,4,128,128]{3,2,1,0:T(8,128)(2,1)S(1)} all-to-all(bf16[8,4,128,128]{3,2,1,0:T(8,128)(2,1)} %get-tuple-element.35), channel_id=1, replica_groups=mesh['span'=16,'sp'=8,'fsdp'=2] {'sp'}, dimensions={0} | all-to-all | bytes 2097152 | tf_op jit(solution)/shard_map/all_to_all | solution.py:289
  28.5 4.7 %all-to-all-start.1 = ((bf16[16,2,128,128]{3,2,1,0:T(8,128)(2,1)}), bf16[16,2,128,128]{3,2,1,0:T(8,128)(2,1)S(1)}, u32[]{:S(2)}, u32[]{:S(2)}) async-start(bf16[16,2,128,128]{3,2,1,0:T(8,128)(2,1)} %get-tuple-element.26), calls=%async_computation.1 | async-start | bytes 2097152 | tf_op jit(solution)/shard_map/all_to_all | solution.py:284
  33.3 0.5 slice.41
  33.8 1.3 fusion.2
  35.7 3.5 %collective-permute-start = (f32[8,128]{1,0:T(8,128)S(1)}, f32[8,128]{1,0:T(8,128)S(1)}, u32[]{:S(2)}, u32[]{:S(2)}) collective-permute-start(f32[8,128]{1,0:T(8,128)S(1)} %broadcast_in_dim.83), channel_id=1, source_target_pairs={{0,16},{16,0},{32,48},{48,32},{64,80},{80,64},{96,112},{112,96},{1... | collective-permute-start | bytes 12296 | tf_op jit(solution)/shard_map/ppermute | solution.py:260
  39.2 10.4 %all-to-all-done.1.ko_ref.vo_ref.kp_ref.vp_ref = bf16[16,2,128,128]{3,2,1,0:T(8,128)(2,1)S(1)} async-done(((bf16[16,2,128,128]{3,2,1,0:T(8,128)(2,1)}), bf16[16,2,128,128]{3,2,1,0:T(8,128)(2,1)S(1)}, u32[]{:S(2)}, u32[]{:S(2)}) %all-to-all-start.1) | async-done | bytes 1048608 | tf_op jit(solution)/shard_map/all_to_all | solution.py:284
  49.6 4.7 %all-to-all-start = ((bf16[16,2,128,128]{3,2,1,0:T(8,128)(2,1)}), bf16[16,2,128,128]{3,2,1,0:T(8,128)(2,1)S(1)}, u32[]{:S(2)}, u32[]{:S(2)}) async-start(bf16[16,2,128,128]{3,2,1,0:T(8,128)(2,1)} %get-tuple-element.25), calls=%async_computation | async-start | bytes 2097152 | tf_op jit(solution)/shard_map/all_to_all | solution.py:284
  54.4 0.2 select_reduce_fusion
  54.7 0.1 pad.4.clone
  54.8 0.5 slice.42
  55.9 0.8 slice.55
  56.8 6.1 %collective-permute-start.3 = (bf16[8,2,128,128]{3,2,1,0:T(8,128)(2,1)}, bf16[8,2,128,128]{3,2,1,0:T(8,128)(2,1)}, u32[]{:S(2)}, u32[]{:S(2)}) collective-permute-start(bf16[8,2,128,128]{3,2,1,0:T(8,128)(2,1)} %slice.55), channel_id=1, source_target_pairs={{0,16},{16,32},{32,48},{48,64},{64,80},{80,96},{96,112},{112,128},... | collective-permute-start | bytes 1572872 | tf_op jit(solution)/shard_map/ppermute | solution.py:256
  62.9 0.7 or_select_fusion
  63.6 3.1 %collective-permute-start.1 = (bf16[8,2,128,128]{3,2,1,0:T(8,128)(2,1)S(1)}, bf16[8,2,128,128]{3,2,1,0:T(8,128)(2,1)S(1)}, u32[]{:S(2)}, u32[]{:S(2)}) collective-permute-start(bf16[8,2,128,128]{3,2,1,0:T(8,128)(2,1)S(1)} %slice.54), channel_id=1, source_target_pairs={{0,32},{16,48},{32,64},{48,80},{64,96},{80,112},{96,128},{112,144}... | collective-permute-start | bytes 1572872 | tf_op jit(solution)/shard_map/ppermute | solution.py:256
  66.7 0.7 select_select_fusion.info_ref
  67.3 3.7 %all-to-all-done.q_ref.g_ref = bf16[16,2,128,128]{3,2,1,0:T(8,128)(2,1)S(1)} async-done(((bf16[16,2,128,128]{3,2,1,0:T(8,128)(2,1)}), bf16[16,2,128,128]{3,2,1,0:T(8,128)(2,1)S(1)}, u32[]{:S(2)}, u32[]{:S(2)}) %all-to-all-start) | async-done | bytes 1048608 | tf_op jit(solution)/shard_map/all_to_all | solution.py:284
  71.0 1.0 copy-done.4
  72.0 10.1 %shard_map.103 = (bf16[1024,128]{1,0:T(8,128)(2,1)}, f32[1024,128]{1,0:T(8,128)}, f32[1024,128]{1,0:T(8,128)}, bf16[2048,128]{1,0:T(8,128)(2,1)}, f32[8,128]{1,0:T(8,128)}) custom-call(s32[3,8]{1,0:T(4,128)} %select_select_fusion.info_ref, bf16[16,2,128,128]{3,2,1,0:T(8,128)(2,1)} %copy-done.4, bf16[16,2,128,128]{3,2,1,0:T(8,128)(2,1)} %copy-done.4, ...), custom_call_target="tpu_custom_call" | custom-call | flops 2684354560 | bytes 3145728 | tf_op jit(solution)/shard_map/pallas_call | solution.py:153
  82.1 10.3 %shard_map.105 = (bf16[1024,128]{1,0:T(8,128)(2,1)}, f32[1024,128]{1,0:T(8,128)}, f32[1024,128]{1,0:T(8,128)}, bf16[2048,128]{1,0:T(8,128)(2,1)}, f32[8,128]{1,0:T(8,128)}) custom-call(s32[3,8]{1,0:T(4,128)} %select_select_fusion.info_ref, bf16[8,4,128,128]{3,2,1,0:T(8,128)(2,1)} %copy-done.3, bf16[8,4,128,128]{3,2,1,0:T(8,128)(2,1)} %copy-done.3, ...), custom_call_target="tpu_custom_call" | custom-call | flops 2684354560 | bytes 3145728 | tf_op jit(solution)/shard_map/pallas_call | solution.py:153
  92.4 0.7 slice.47
  93.1 0.8 copy-done.12
  93.9 10.1 %shard_map.102 = (bf16[1024,128]{1,0:T(8,128)(2,1)}, f32[1024,128]{1,0:T(8,128)}, f32[1024,128]{1,0:T(8,128)}, bf16[2048,128]{1,0:T(8,128)(2,1)}, f32[8,128]{1,0:T(8,128)}) custom-call(s32[3,8]{1,0:T(4,128)} %select_select_fusion.info_ref, bf16[16,2,128,128]{3,2,1,0:T(8,128)(2,1)} %copy-done.4, bf16[16,2,128,128]{3,2,1,0:T(8,128)(2,1)} %copy-done.4, ...), custom_call_target="tpu_custom_call" | custom-call | flops 2684354560 | bytes 3145728 | tf_op jit(solution)/shard_map/pallas_call | solution.py:153
  104.0 0.7 slice_add_fusion.1
  104.8 1.3 collective-permute-start.4
  106.2 13.8 %collective-permute-start.6 = (f32[8,128]{1,0:T(8,128)S(1)}, f32[8,128]{1,0:T(8,128)S(1)}, u32[]{:S(2)}, u32[]{:S(2)}) collective-permute-start(f32[8,128]{1,0:T(8,128)S(1)} %fusion.3), channel_id=1, source_target_pairs={{0,32},{16,48},{32,0},{48,16},{64,96},{80,112},{96,64},{112,80},{1... | collective-permute-start | bytes 12296 | tf_op jit(solution)/shard_map/ppermute | solution.py:260
  120.0 12.5 %collective-permute-done.6 = f32[8,128]{1,0:T(8,128)S(1)} collective-permute-done((f32[8,128]{1,0:T(8,128)S(1)}, f32[8,128]{1,0:T(8,128)S(1)}, u32[]{:S(2)}, u32[]{:S(2)}) %collective-permute-start.6) | collective-permute-done | bytes 4128 | tf_op jit(solution)/shard_map/ppermute | solution.py:260
  132.6 3.5 %collective-permute-start.7 = (f32[8,128]{1,0:T(8,128)S(1)}, f32[8,128]{1,0:T(8,128)S(1)}, u32[]{:S(2)}, u32[]{:S(2)}) collective-permute-start(f32[8,128]{1,0:T(8,128)S(1)} %fusion.4), channel_id=1, source_target_pairs={{0,64},{16,80},{32,96},{48,112},{64,0},{80,16},{96,32},{112,48},{1... | collective-permute-start | bytes 12296 | tf_op jit(solution)/shard_map/ppermute | solution.py:260
  136.1 1.6 collective-permute-done.7
  137.7 6.2 %collective-permute-start.8 = (f32[8,128]{1,0:T(8,128)S(1)}, f32[8,128]{1,0:T(8,128)S(1)}, u32[]{:S(2)}, u32[]{:S(2)}) collective-permute-start(f32[8,128]{1,0:T(8,128)S(1)} %add.83), channel_id=1, source_target_pairs={{0,128},{16,144},{32,160},{48,176},{64,192},{80,208},{96,224},{112... | collective-permute-start | bytes 12296 | tf_op jit(solution)/shard_map/ppermute | solution.py:260
  143.9 1.6 collective-permute-done.8
  145.5 0.6 broadcast_in_dim.95
  146.1 3.5 %all-to-all-start.5 = ((f32[16,8,128]{2,1,0:T(8,128)}), f32[16,8,128]{2,1,0:T(8,128)S(1)}, u32[]{:S(2)}, u32[]{:S(2)}) async-start(f32[16,8,128]{2,1,0:T(8,128)} %broadcast_in_dim.95), calls=%async_computation.5 | async-start | bytes 131072 | tf_op jit(solution)/shard_map/all_to_all | solution.py:284
  149.6 0.8 copy-done.5
  150.4 2.5 %shard_map.106 = bf16[8,384,128]{2,1,0:T(8,128)(2,1)} custom-call(bf16[1024,128]{1,0:T(8,128)(2,1)} %get-tuple-element.36.refs_0_, f32[1024,128]{1,0:T(8,128)} %get-tuple-element.37.refs_1_, f32[1024,128]{1,0:T(8,128)} %get-tuple-element.38.refs_2_, bf16[2048,128]{1,0:T(8,128)(2,1)} %copy-done.5), custom_call_target="tpu_custom_call" | custom-call | flops 1310720 | bytes 2621440 | tf_op jit(solution)/shard_map/pallas_call | solution.py:199
  152.9 4.3 %all-to-all-done.5 = f32[16,8,128]{2,1,0:T(8,128)S(1)} async-done(((f32[16,8,128]{2,1,0:T(8,128)}), f32[16,8,128]{2,1,0:T(8,128)S(1)}, u32[]{:S(2)}, u32[]{:S(2)}) %all-to-all-start.5) | async-done | bytes 65568 | tf_op jit(solution)/shard_map/all_to_all | solution.py:284
  157.2 3.5 %all-to-all-start.4 = ((bf16[8,384,128]{2,1,0:T(8,128)(2,1)}), bf16[8,384,128]{2,1,0:T(8,128)(2,1)S(1)}, u32[]{:S(2)}, u32[]{:S(2)}) async-start(bf16[8,384,128]{2,1,0:T(8,128)(2,1)} %shard_map.106), calls=%async_computation.4 | async-start | bytes 1572864 | tf_op jit(solution)/shard_map/all_to_all | solution.py:289
  160.8 1.3 collective-permute-start.2
  162.1 10.9 %collective-permute-done.2.refs_7_ = bf16[2048,128]{1,0:T(8,128)(2,1)S(1)} collective-permute-done((bf16[2048,128]{1,0:T(8,128)(2,1)S(1)}, bf16[2048,128]{1,0:T(8,128)(2,1)S(1)}, u32[]{:S(2)}, u32[]{:S(2)}) %collective-permute-start.2) | collective-permute-done | bytes 524320 | tf_op jit(solution)/shard_map/ppermute | solution.py:256
  173.0 0.8 copy-done.6
  173.8 3.4 %shard_map.104 = bf16[16,384,128]{2,1,0:T(8,128)(2,1)} custom-call(bf16[1024,128]{1,0:T(8,128)(2,1)} %get-tuple-element.27.refs_0_, f32[1024,128]{1,0:T(8,128)} %get-tuple-element.28.refs_1_, f32[1024,128]{1,0:T(8,128)} %get-tuple-element.29.refs_2_, bf16[2048,128]{1,0:T(8,128)(2,1)} %get-tuple-element.30.refs_3_, ...), custom_call_target="tpu_custom_call" | custom-call | flops 2621440 | bytes 5242880 | tf_op jit(solution)/shard_map/pallas_call | solution.py:199
  177.2 0.9 copy-done.1
  178.1 5.4 %all-to-all-start.2 = ((bf16[16,384,128]{2,1,0:T(8,128)(2,1)}), bf16[16,384,128]{2,1,0:T(8,128)(2,1)S(1)}, u32[]{:S(2)}, u32[]{:S(2)}) async-start(bf16[16,384,128]{2,1,0:T(8,128)(2,1)} %shard_map.104), calls=%async_computation.2 | async-start | bytes 3145728 | tf_op jit(solution)/shard_map/all_to_all | solution.py:284
  183.7 0.6 broadcast_divide_fusion
  184.3 18.4 %all-to-all-done.2.refs_0_.refs_1_.refs_2_ = bf16[16,384,128]{2,1,0:T(8,128)(2,1)S(1)} async-done(((bf16[16,384,128]{2,1,0:T(8,128)(2,1)}), bf16[16,384,128]{2,1,0:T(8,128)(2,1)S(1)}, u32[]{:S(2)}, u32[]{:S(2)}) %all-to-all-start.2) | async-done | bytes 1572896 | tf_op jit(solution)/shard_map/all_to_all | solution.py:284
  202.7 1.2 copy-done
  203.9 4.8 %finish.1 = (bf16[128,3072]{1,0:T(8,128)(2,1)}, bf16[128,3072]{1,0:T(8,128)(2,1)}, bf16[128,3072]{1,0:T(8,128)(2,1)}) custom-call(bf16[128,3072]{1,0:T(8,128)(2,1)} %bitcast.19, bf16[128,3072]{1,0:T(8,128)(2,1)} %bitcast.21, f32[2,3072]{1,0:T(2,128)} %all_gather.3.gain_ref, bf16[16,384,128]{2,1,0:T(8,128)(2,1)} %copy-done, bf16[16,384,128]{2,1,0:T(8,128)(2,1)} %copy-done, ...), custom_call_target="tpu_custom_call" | custom-call | flops 11796480 | bytes 6291456 | tf_op jit(solution)/shard_map/finish/pallas_call | solution.py:239
  (43 shorter events, 0.5 us)
Async XLA Ops:
  28.5 27.4 %copy-start.3 = (bf16[8,4,128,128]{3,2,1,0:T(8,128)(2,1)}, bf16[8,4,128,128]{3,2,1,0:T(8,128)(2,1)S(1)}, u32[]{:S(2)}) copy-start(bf16[8,4,128,128]{3,2,1,0:T(8,128)(2,1)S(1)} %all_to_all.30.q_ref.g_ref.ko_ref.vo_ref) | copy-start | bytes 3145732
  28.5 4.7 %copy-start.8 = (s32[1,1024]{1,0:T(1,128)S(1)}, s32[1,1024]{1,0:T(1,128)}, u32[]{:S(2)}) copy-start(s32[1,1024]{1,0:T(1,128)} %param.12) | copy-start | bytes 12292
  28.5 21.1 %all-to-all-start.1 = ((bf16[16,2,128,128]{3,2,1,0:T(8,128)(2,1)}), bf16[16,2,128,128]{3,2,1,0:T(8,128)(2,1)S(1)}, u32[]{:S(2)}, u32[]{:S(2)}) async-start(bf16[16,2,128,128]{3,2,1,0:T(8,128)(2,1)} %get-tuple-element.26), calls=%async_computation.1 | async-start | bytes 2097152 | tf_op jit(solution)/shard_map/all_to_all | solution.py:284
  33.3 21.2 %copy-start.9 = (s32[1,32]{1,0:T(1,128)S(1)}, s32[1,32]{1,0:T(1,128)}, u32[]{:S(2)}) copy-start(s32[1,32]{1,0:T(1,128)} %param.13) | copy-start | bytes 388
  35.7 19.0 %collective-permute-start = (f32[8,128]{1,0:T(8,128)S(1)}, f32[8,128]{1,0:T(8,128)S(1)}, u32[]{:S(2)}, u32[]{:S(2)}) collective-permute-start(f32[8,128]{1,0:T(8,128)S(1)} %broadcast_in_dim.83), channel_id=1, source_target_pairs={{0,16},{16,0},{32,48},{48,32},{64,80},{80,64},{96,112},{112,96},{1... | collective-permute-start | bytes 12296 | tf_op jit(solution)/shard_map/ppermute | solution.py:260
  49.6 13.9 %copy-start.2 = (bf16[16,2,128,128]{3,2,1,0:T(8,128)(2,1)}, bf16[16,2,128,128]{3,2,1,0:T(8,128)(2,1)S(1)}, u32[]{:S(2)}) copy-start(bf16[16,2,128,128]{3,2,1,0:T(8,128)(2,1)S(1)} %all-to-all-done.1.ko_ref.vo_ref.kp_ref.vp_ref) | copy-start | bytes 3145732
  49.6 21.4 %all-to-all-start = ((bf16[16,2,128,128]{3,2,1,0:T(8,128)(2,1)}), bf16[16,2,128,128]{3,2,1,0:T(8,128)(2,1)S(1)}, u32[]{:S(2)}, u32[]{:S(2)}) async-start(bf16[16,2,128,128]{3,2,1,0:T(8,128)(2,1)} %get-tuple-element.25), calls=%async_computation | async-start | bytes 2097152 | tf_op jit(solution)/shard_map/all_to_all | solution.py:284
  56.8 25.4 %collective-permute-start.3 = (bf16[8,2,128,128]{3,2,1,0:T(8,128)(2,1)}, bf16[8,2,128,128]{3,2,1,0:T(8,128)(2,1)}, u32[]{:S(2)}, u32[]{:S(2)}) collective-permute-start(bf16[8,2,128,128]{3,2,1,0:T(8,128)(2,1)} %slice.55), channel_id=1, source_target_pairs={{0,16},{16,32},{32,48},{48,64},{64,80},{80,96},{96,112},{112,128},... | collective-permute-start | bytes 1572872 | tf_op jit(solution)/shard_map/ppermute | solution.py:256
  63.6 29.5 %collective-permute-start.1 = (bf16[8,2,128,128]{3,2,1,0:T(8,128)(2,1)S(1)}, bf16[8,2,128,128]{3,2,1,0:T(8,128)(2,1)S(1)}, u32[]{:S(2)}, u32[]{:S(2)}) collective-permute-start(bf16[8,2,128,128]{3,2,1,0:T(8,128)(2,1)S(1)} %slice.54), channel_id=1, source_target_pairs={{0,32},{16,48},{32,64},{48,80},{64,96},{80,112},{96,128},{112,144}... | collective-permute-start | bytes 1572872 | tf_op jit(solution)/shard_map/ppermute | solution.py:256
  71.0 1.0 copy-start.4
  93.1 11.7 %copy-start.11 = (bf16[2048,128]{1,0:T(8,128)(2,1)S(1)}, bf16[2048,128]{1,0:T(8,128)(2,1)}, u32[]{:S(2)}) copy-start(bf16[2048,128]{1,0:T(8,128)(2,1)} %get-tuple-element.39) | copy-start | bytes 1572868
  93.1 0.8 copy-start.12
  104.8 1.4 collective-permute-start.5
  104.8 44.8 %collective-permute-start.4 = (bf16[2048,128]{1,0:T(8,128)(2,1)S(1)}, bf16[2048,128]{1,0:T(8,128)(2,1)S(1)}, u32[]{:S(2)}, u32[]{:S(2)}) collective-permute-start(bf16[2048,128]{1,0:T(8,128)(2,1)S(1)} %copy-done.11), channel_id=1, source_target_pairs={{16,0},{32,16},{48,32},{64,48},{80,64},{96,80},{112,96},{128,112},... | collective-permute-start | bytes 1572872 | tf_op jit(solution)/shard_map/ppermute | solution.py:256
  106.2 26.3 %collective-permute-start.6 = (f32[8,128]{1,0:T(8,128)S(1)}, f32[8,128]{1,0:T(8,128)S(1)}, u32[]{:S(2)}, u32[]{:S(2)}) collective-permute-start(f32[8,128]{1,0:T(8,128)S(1)} %fusion.3), channel_id=1, source_target_pairs={{0,32},{16,48},{32,0},{48,16},{64,96},{80,112},{96,64},{112,80},{1... | collective-permute-start | bytes 12296 | tf_op jit(solution)/shard_map/ppermute | solution.py:260
  132.6 5.1 %collective-permute-start.7 = (f32[8,128]{1,0:T(8,128)S(1)}, f32[8,128]{1,0:T(8,128)S(1)}, u32[]{:S(2)}, u32[]{:S(2)}) collective-permute-start(f32[8,128]{1,0:T(8,128)S(1)} %fusion.4), channel_id=1, source_target_pairs={{0,64},{16,80},{32,96},{48,112},{64,0},{80,16},{96,32},{112,48},{1... | collective-permute-start | bytes 12296 | tf_op jit(solution)/shard_map/ppermute | solution.py:260
  137.7 7.7 %collective-permute-start.8 = (f32[8,128]{1,0:T(8,128)S(1)}, f32[8,128]{1,0:T(8,128)S(1)}, u32[]{:S(2)}, u32[]{:S(2)}) collective-permute-start(f32[8,128]{1,0:T(8,128)S(1)} %add.83), channel_id=1, source_target_pairs={{0,128},{16,144},{32,160},{48,176},{64,192},{80,208},{96,224},{112... | collective-permute-start | bytes 12296 | tf_op jit(solution)/shard_map/ppermute | solution.py:260
  146.1 11.1 %all-to-all-start.5 = ((f32[16,8,128]{2,1,0:T(8,128)}), f32[16,8,128]{2,1,0:T(8,128)S(1)}, u32[]{:S(2)}, u32[]{:S(2)}) async-start(f32[16,8,128]{2,1,0:T(8,128)} %broadcast_in_dim.95), calls=%async_computation.5 | async-start | bytes 131072 | tf_op jit(solution)/shard_map/all_to_all | solution.py:284
  149.6 0.8 copy-start.5
  150.4 10.4 %copy-start.10 = (bf16[2048,128]{1,0:T(8,128)(2,1)S(1)}, bf16[2048,128]{1,0:T(8,128)(2,1)}, u32[]{:S(2)}) copy-start(bf16[2048,128]{1,0:T(8,128)(2,1)} %get-tuple-element.34) | copy-start | bytes 1572868
  157.2 20.0 %all-to-all-start.4 = ((bf16[8,384,128]{2,1,0:T(8,128)(2,1)}), bf16[8,384,128]{2,1,0:T(8,128)(2,1)S(1)}, u32[]{:S(2)}, u32[]{:S(2)}) async-start(bf16[8,384,128]{2,1,0:T(8,128)(2,1)} %shard_map.106), calls=%async_computation.4 | async-start | bytes 1572864 | tf_op jit(solution)/shard_map/all_to_all | solution.py:289
  160.8 12.2 %collective-permute-start.2 = (bf16[2048,128]{1,0:T(8,128)(2,1)S(1)}, bf16[2048,128]{1,0:T(8,128)(2,1)S(1)}, u32[]{:S(2)}, u32[]{:S(2)}) collective-permute-start(bf16[2048,128]{1,0:T(8,128)(2,1)S(1)} %copy-done.10), channel_id=1, source_target_pairs={{32,0},{48,16},{64,32},{80,48},{96,64},{112,80},{128,96},{144,112}... | collective-permute-start | bytes 1572872 | tf_op jit(solution)/shard_map/ppermute | solution.py:256
  173.0 0.8 copy-start.6
  177.2 6.4 %copy-start.7 = (f32[2,1536]{1,0:T(2,128)S(1)}, f32[2,1536]{1,0:T(2,128)}, u32[]{:S(2)}) copy-start(f32[2,1536]{1,0:T(2,128)} %param.11) | copy-start | bytes 36868
  177.2 0.9 copy-start.1
  178.1 24.6 %all-to-all-start.2 = ((bf16[16,384,128]{2,1,0:T(8,128)(2,1)}), bf16[16,384,128]{2,1,0:T(8,128)(2,1)S(1)}, u32[]{:S(2)}, u32[]{:S(2)}) async-start(bf16[16,384,128]{2,1,0:T(8,128)(2,1)} %shard_map.104), calls=%async_computation.2 | async-start | bytes 3145728 | tf_op jit(solution)/shard_map/all_to_all | solution.py:284
  202.7 1.2 copy-start
